TPU v7x, 32 devices: a whole 2x2x4 slice. The times are simulated.
32 devices in a mesh: cand: 4 (over x, core), seq: 8 (over z, y).
Axes of the slice: x: 2, y: 2, z: 4, core: 2. Of those that a mesh axis runs over, the one named last changes fastest.
Arguments:
- latent: bfloat16 [4, 384, 3072], P('cand', 'seq'), may hold values from -0.59765625 to 0.59765625
- timesteps: int32 [4], replicated, may hold values from 0 to 999
- positions: int32 [3, 384], replicated, may hold values from 0 to 63
- mod_weight: bfloat16 [3072, 9216], P('cand', 'seq'), may hold values from -0.109375 to 0.109375
- input_weight: bfloat16 [3072, 16, 384], P('cand', 'seq'), may hold values from -0.109375 to 0.109375
- output_weight: bfloat16 [16, 128, 3072], P('seq', None, 'cand'), may hold values from -0.75 to 0.75
- cotangent: bfloat16 [4, 384, 3072], P('cand', 'seq'), may hold values from -6 to 6
Outputs:
- block_out: bfloat16 [4, 384, 3072], P('cand', 'seq')
- latent_grad: float32 [4, 384, 3072], P('cand', 'seq')
All inputs are finite; a program needn't handle non-finite values.
Results may differ from a plain program's by a relative error of at most 0.033.
Values may be sent and summed in bfloat16 or wider, within the bound.
A program may use at most 128 MiB of HBM per device.

v0:
```python
import jax
import jax.numpy as jnp
import numpy as np
from jax import lax
from jax.sharding import PartitionSpec as P

HEAD = 128


epsilon = 1e-06


def time_embed(timesteps, feature_width):
    half_size = feature_width // 2
    freq_rate = jnp.exp(-jnp.log(10000.0) * jnp.arange(half_size, dtype=jnp.float32) / half_size)
    angles = timesteps.astype(jnp.float32)[:, None] * freq_rate[None, :]
    return jnp.concatenate([jnp.cos(angles), jnp.sin(angles)], axis=1)


def rope_tables(positions, head_size):
    first_size = head_size // 8
    other_size = (head_size - first_size) // 2
    pieces = []
    swapped = []
    sign_vec = []
    offset = 0
    for axis_id, width_part in enumerate((first_size, other_size, other_size)):
        half_size = width_part // 2
        freq_rate = jnp.exp(
            -jnp.log(256.0) * 2.0 * jnp.arange(half_size, dtype=jnp.float32) / width_part
        )
        angle_part = positions[axis_id].astype(jnp.float32)[:, None] * freq_rate[None, :]
        pieces.append(angle_part)
        pieces.append(angle_part)
        swapped += list(range(offset + half_size, offset + width_part)) + list(
            range(offset, offset + half_size)
        )
        sign_vec += [-1.0] * half_size + [1.0] * half_size
        offset += width_part
    angles = jnp.concatenate(pieces, axis=1)
    return (
        jnp.cos(angles),
        jnp.sin(angles),
        np.array(swapped, np.int32),
        np.array(sign_vec, np.float32),
    )


def rotate(values, tables):
    cos_tab, sin_tab, swapped, sign_vec = tables
    return values * cos_tab + values[..., swapped] * sign_vec * sin_tab


def unrotate(values, tables):
    cos_tab, sin_tab, swapped, sign_vec = tables
    return values * cos_tab - (values * sin_tab)[..., swapped] * sign_vec


def rms_norm(values):
    inverse = lax.rsqrt(jnp.mean(values * values, -1, keepdims=True) + epsilon)
    return (values * inverse, inverse)


def rms_back(d_normed, normed, inverse):
    return inverse * (d_normed - normed * jnp.mean(d_normed * normed, -1, keepdims=True))


def layer_norm(values):
    centred = values - jnp.mean(values, -1, keepdims=True)
    inverse_std = lax.rsqrt(jnp.mean(centred * centred, -1, keepdims=True) + epsilon)
    return (centred * inverse_std, inverse_std)


def layer_norm_back(d_normed, normed, inverse_std):
    return inverse_std * (
        d_normed
        - jnp.mean(d_normed, -1, keepdims=True)
        - normed * jnp.mean(d_normed * normed, -1, keepdims=True)
    )


def times_transposed(left, right):
    return lax.dot_general(
        left, right, (((1,), (1,)), ((), ())), preferred_element_type=jnp.float32
    )


def attend(projected, tables):
    length, groups, triple = projected.shape
    head_size = triple // 3
    grouped = jnp.transpose(projected.reshape(length, groups, 3, head_size), (2, 1, 0, 3))
    query_n, query_inv = rms_norm(grouped[0])
    key_n, key_inv = rms_norm(grouped[1])
    q_rot = rotate(query_n, tables).astype(jnp.bfloat16)
    k_rot = rotate(key_n, tables).astype(jnp.bfloat16)
    values = grouped[2].astype(jnp.bfloat16)
    score_scale = head_size ** (-0.5)
    scores = (
        jnp.einsum("gld,gmd->glm", q_rot, k_rot, preferred_element_type=jnp.float32) * score_scale
    )
    weights = jnp.exp(scores - head_size**0.5)
    probs = weights / jnp.sum(weights, -1, keepdims=True)
    probs_low = probs.astype(jnp.bfloat16)
    heads_out = jnp.einsum("glm,gmd->gld", probs_low, values, preferred_element_type=jnp.float32)
    attended = (
        jnp.transpose(heads_out, (1, 0, 2)).reshape(length, groups * head_size).astype(jnp.bfloat16)
    )
    saved = (q_rot, k_rot, values, probs, probs_low, query_n, query_inv, key_n, key_inv)
    return (attended, saved)


def attend_back(d_attended, saved, tables):
    q_rot, k_rot, values, probs, probs_low, query_n, query_inv, key_n, key_inv = saved
    groups, length, head_size = q_rot.shape
    score_scale = head_size ** (-0.5)
    d_heads = jnp.transpose(d_attended.reshape(length, groups, head_size), (1, 0, 2))
    d_values = jnp.einsum("glm,gld->gmd", probs_low, d_heads, preferred_element_type=jnp.float32)
    d_probs = jnp.einsum("gld,gmd->glm", d_heads, values, preferred_element_type=jnp.float32)
    d_scores = (probs * (d_probs - jnp.sum(probs * d_probs, -1, keepdims=True))).astype(
        jnp.bfloat16
    )
    d_qrot = (
        jnp.einsum("glm,gmd->gld", d_scores, k_rot, preferred_element_type=jnp.float32)
        * score_scale
    )
    d_krot = (
        jnp.einsum("glm,gld->gmd", d_scores, q_rot, preferred_element_type=jnp.float32)
        * score_scale
    )
    d_query = rms_back(unrotate(d_qrot, tables), query_n, query_inv)
    d_key = rms_back(unrotate(d_krot, tables), key_n, key_inv)
    stacked = jnp.stack([d_query, d_key, d_values], 0)
    return (
        jnp.transpose(stacked, (2, 1, 0, 3))
        .reshape(length, groups * 3 * head_size)
        .astype(jnp.bfloat16)
    )


def on_device(latent, timesteps, positions, mod_weight, input_weight, output_weight, cotangent):
    width = latent.shape[2]
    rows_local = latent.shape[1]
    groups = input_weight.shape[1]
    group_cols = groups * input_weight.shape[2]
    time_act = jax.nn.silu(time_embed(timesteps, width)).astype(jnp.bfloat16)
    slab_rows = mod_weight.shape[0]
    act_rows = lax.dynamic_slice_in_dim(time_act, lax.axis_index("cand") * slab_rows, slab_rows, 1)
    mod_mine = lax.psum_scatter(
        jnp.dot(act_rows, mod_weight, preferred_element_type=jnp.float32).astype(jnp.bfloat16),
        "cand",
        scatter_dimension=0,
        tiled=True,
    ).astype(jnp.float32)
    modulation = lax.all_gather(mod_mine, "seq", axis=1, tiled=True)[0]
    shift_vec = modulation[:width]
    scale_vec = modulation[width : 2 * width]
    gate_vec = modulation[2 * width :]
    latent_rows = latent[0].astype(jnp.float32)
    normed, inverse_std = layer_norm(latent_rows)
    modulated = (normed * (1.0 + scale_vec) + shift_vec).astype(jnp.bfloat16)
    gathered = lax.all_gather(modulated, "seq", axis=0, tiled=True)
    length = gathered.shape[0]
    tables = rope_tables(positions, HEAD)
    piece = lax.all_gather(input_weight, "cand", axis=0, tiled=True)
    projected = jnp.dot(
        gathered, piece.reshape(piece.shape[0], group_cols), preferred_element_type=jnp.float32
    )
    attended, saved = attend(projected.reshape(length, groups, 3 * HEAD), tables)
    w_heads = lax.all_gather(output_weight, "seq", axis=0, tiled=True)
    w_all = lax.all_gather(w_heads, "cand", axis=2, tiled=True)
    w_all = w_all.reshape(w_all.shape[0] * w_all.shape[1], width)
    token_heads = lax.all_to_all(attended, "seq", split_axis=0, concat_axis=1, tiled=True)
    mixed = jnp.dot(token_heads, w_all, preferred_element_type=jnp.float32)
    block_out = (latent_rows + gate_vec * mixed).astype(jnp.bfloat16)
    d_mixed = (cotangent[0].astype(jnp.float32) * gate_vec).astype(jnp.bfloat16)
    d_tokens = times_transposed(d_mixed, w_all).astype(jnp.bfloat16)
    d_attended = lax.all_to_all(d_tokens, "seq", split_axis=1, concat_axis=0, tiled=True)
    d_projected = attend_back(d_attended, saved, tables)
    w_back = lax.all_gather(input_weight, "cand", axis=0, tiled=True).reshape(width, group_cols)
    d_modulated = lax.psum_scatter(
        times_transposed(
            lax.slice_in_dim(d_projected, 0, rows_local * lax.axis_size("seq"), axis=0), w_back
        ).astype(jnp.bfloat16),
        "seq",
        scatter_dimension=0,
        tiled=True,
    ).astype(jnp.float32)
    latent_grad = cotangent[0].astype(jnp.float32) + layer_norm_back(
        d_modulated * (1.0 + scale_vec), normed, inverse_std
    )
    return (block_out[None], latent_grad[None])


def solution(mesh):
    placed = (
        P("cand", "seq", None),
        P(),
        P(),
        P("cand", "seq"),
        P("cand", "seq", None),
        P("seq", None, "cand"),
        P("cand", "seq", None),
    )
    return jax.shard_map(
        on_device,
        mesh=mesh,
        in_specs=placed,
        out_specs=(P("cand", "seq", None), P("cand", "seq", None)),
        check_vma=False,
    )
```

profile of v0, /device:TPU:0, one launch (start us, length us, event | category | flops | bytes accessed | tf_op | source)
XLA Modules:
  0.0 380.3 jit_solution(16041550091423698796)
XLA Ops:
  10.0 8.7 %all-reduce = bf16[4,1152]{1,0:T(4,128)(2,1)S(1)} all-reduce(bf16[4,1152]{1,0:T(4,128)(2,1)S(1)} %convolution_convert_fusion.2), channel_id=2, replica_groups=mesh['cand'=4,'seq'=8] {'cand'}, use_global_device_ids=true, to_apply=%region_0.1.clone | all-reduce | flops 4608 | bytes 18432
  19.4 31.6 %all_gather.16 = f32[1,9216]{1,0:T(1,128)S(1)} all-gather(f32[1,1152]{1,0:T(1,128)S(1)} %dynamic-slice_convert_fusion), channel_id=1, replica_groups=mesh['cand'=4,'seq'=8] {'seq'}, dimensions={1}, use_global_device_ids=true | all-gather | bytes 41472 | tf_op jit(solution)/shard_map/all_gather | solution.py:154
  52.4 20.8 %all-gather.9.cloned.1.call-done = bf16[16,128,768]{2,1,0:T(8,128)(2,1)} async-done(((bf16[2,128,768]{2,1,0:T(8,128)(2,1)}), bf16[16,128,768]{2,1,0:T(8,128)(2,1)}) %all-gather.9.cloned.1.call-update) | async-done | bytes 3145744 | tf_op jit(solution)/shard_map/all_gather | solution.py:169
  76.4 34.5 %all-gather.7.cloned.1.call-done = bf16[3072,2,384]{2,1,0:T(2,128)(2,1)} async-done(((bf16[768,2,384]{2,1,0:T(2,128)(2,1)}), bf16[3072,2,384]{2,1,0:T(2,128)(2,1)}) %all-gather.7.cloned.1.call-update) | async-done | bytes 4718608 | tf_op jit(solution)/shard_map/all_gather | solution.py:164
  110.9 5.2 %copy.89 = bf16[384,8,2,384]{3,1,2,0:T(8,128)(2,1)} copy(bf16[384,8,2,384]{3,2,1,0:T(2,128)(2,1)} %bitcast.149) | data formatting | bytes 9437184
  116.1 6.7 %copy.50 = bf16[3072,768]{0,1:T(8,128)(2,1)} copy(bf16[3072,768]{1,0:T(8,128)(2,1)} %bitcast.145) | data formatting | bytes 9437184 | tf_op jit(solution)/shard_map/reshape | solution.py:166
  122.8 42.7 %all-gather.5.cloned.1.call-done = bf16[384,3072]{1,0:T(8,128)(2,1)} async-done(((bf16[48,3072]{1,0:T(8,128)(2,1)}), bf16[384,3072]{1,0:T(8,128)(2,1)}) %all-gather.5.cloned.1.call-update) | async-done | bytes 2359312 | tf_op jit(solution)/shard_map/all_gather | solution.py:161
  165.5 5.3 %fusion.5 = f32[3,2,384,128]{2,3,0,1:T(8,128)S(1)} fusion(bf16[2,3,128,3072]{3,2,1,0:T(8,128)(2,1)} %bitcast.150, bf16[384,3072]{1,0:T(8,128)(2,1)} %all-gather.5.cloned.1.call-done), kind=kOutput, calls=%fused_computation.13 | convolution fusion | flops 1811939328 | bytes 8257536 | tf_op jit(solution)/shard_map/dot_general | solution.py:165
  171.9 75.6 %all-gather.11.cloned.1.call-done = bf16[16,128,3072]{2,1,0:T(8,128)(2,1)} async-done(((bf16[16,128,768]{2,1,0:T(8,128)(2,1)}), bf16[16,128,3072]{2,1,0:T(8,128)(2,1)}) %all-gather.11.cloned.1.call-update) | async-done | bytes 12582928 | tf_op jit(solution)/shard_map/all_gather | solution.py:170
  247.6 8.5 %convolution_convert_fusion.1 = bf16[48,2048]{1,0:T(8,128)(2,1)S(1)} fusion(bf16[2048,3072]{1,0:T(8,128)(2,1)} %bitcast.143, bf16[1,48,3072]{2,1,0:T(8,128)(2,1)S(1)} %copy-done.10, f32[3072]{0:T(1024)S(1)} %bitcast.159), kind=kOutput, calls=%fused_computation.11 | convolution fusion | flops 604520448 | bytes 13086720 | tf_op jit(solution)/shard_map/dot_general | solution.py:83
  256.7 5.5 %all-to-all-start.1 = ((bf16[48,8,256]{2,0,1:T(8,128)(2,1)}), bf16[48,8,256]{2,0,1:T(8,128)(2,1)S(1)}, u32[]{:S(2)}, u32[]{:S(2)}) async-start(bf16[48,8,256]{2,0,1:T(8,128)(2,1)} %bitcast.142), calls=%async_computation.1 | async-start | bytes 393216 | tf_op jit(solution)/shard_map/all_to_all | solution.py:177
  262.5 1.2 fusion.35
  263.7 1.1 copy.52
  265.8 2.2 gather_fusion
  268.0 2.9 gather_fusion.1
  270.9 1.9 fusion.31
  272.9 2.5 fusion.45
  275.3 2.1 multiply_reduce_fusion
  277.5 1.1 fusion.11
  280.7 1.1 broadcast_multiply_fusion
  282.8 2.9 gather_fusion.3
  285.7 2.0 copy.66
  287.8 2.9 gather_fusion.2
  290.6 2.0 multiply_reduce_fusion.2
  292.7 2.0 fusion.41
  294.9 3.5 convolution_convert_fusion
  298.4 1.4 fusion.10
  300.2 18.7 %all_to_all.32 = bf16[8,48,256]{2,1,0:T(8,128)(2,1)S(1)} all-to-all(bf16[8,48,256]{2,1,0:T(8,128)(2,1)S(1)} %convert_element_type.131), channel_id=1, replica_groups=mesh['cand'=4,'seq'=8] {'seq'}, dimensions={0} | all-to-all | bytes 393216 | tf_op jit(solution)/shard_map/all_to_all | solution.py:172
  319.0 7.9 %fusion.2 = bf16[1,48,3072]{2,1,0:T(8,128)(2,1)} fusion(bf16[48,2048]{1,0:T(8,128)(2,1)S(1)} %bitcast.151, bf16[2048,3072]{1,0:T(8,128)(2,1)} %bitcast.144, bf16[1,48,3072]{2,1,0:T(8,128)(2,1)S(1)} %copy-done.2, f32[3072]{0:T(1024)S(1)} %bitcast.160), kind=kOutput, calls=%fused_computation.8 | convolution fusion | flops 604569600 | bytes 13381632 | tf_op jit(solution)/shard_map/dot_general | solution.py:173
  326.9 43.6 %reduce-scatter.2.cloned.1.call-done = bf16[48,3072]{1,0:T(8,128)(2,1)} async-done(((bf16[384,3072]{1,0:T(8,128)(2,1)}), bf16[48,3072]{1,0:T(8,128)(2,1)}) %reduce-scatter.2.cloned.1.call-update) | async-done | bytes 294928 | tf_op jit(solution)/shard_map/reduce_scatter | solution.py:180
  370.5 1.2 fusion.27
  371.8 2.0 fusion.24
  (112 shorter events, 14.9 us)
Async XLA Ops:
  7.2 2.5 copy-start
  7.2 1.6 copy-start.28
  7.2 1.6 copy-start.27
  7.2 66.0 %all-gather.9.cloned.1.call-start = ((), (), s32[]{:S(2)}) async-start(), calls=%async_computation.5 | async-start | bytes 3538944 | tf_op jit(solution)/shard_map/all_gather | solution.py:169
  7.9 103.0 %all-gather.7.cloned.1.call-start = ((), (), s32[]{:S(2)}) async-start(), calls=%async_computation.4 | async-start | bytes 5898240 | tf_op jit(solution)/shard_map/all_gather | solution.py:164
  8.7 42.3 %copy-start.1 = (bf16[1,48,3072]{2,1,0:T(8,128)(2,1)S(1)}, bf16[1,48,3072]{2,1,0:T(8,128)(2,1)}, u32[]{:S(2)}) copy-start(bf16[1,48,3072]{2,1,0:T(8,128)(2,1)} %param.13) | copy-start | bytes 884740
  8.7 156.8 %all-gather.5.cloned.1.call-start = ((), (), s32[]{:S(2)}) async-start(), calls=%async_computation.3 | async-start | bytes 2654208 | tf_op jit(solution)/shard_map/all_gather | solution.py:161
  51.1 22.1 %copy-start.20 = (f32[48]{0:T(128)}, f32[48]{0:T(128)S(1)}, u32[]{:S(2)}) copy-start(f32[48]{0:T(128)S(1)} %broadcast_multiply_fusion.11) | copy-start | bytes 580
  51.4 21.8 %copy-start.23 = (f32[48]{0:T(128)}, f32[48]{0:T(128)S(1)}, u32[]{:S(2)}) copy-start(f32[48]{0:T(128)S(1)} %add_rsqrt_fusion.2) | copy-start | bytes 580
  51.4 196.1 %copy-start.16 = (f32[1,3072]{1,0:T(1,128)}, f32[1,3072]{1,0:T(1,128)S(1)}, u32[]{:S(2)}) copy-start(f32[1,3072]{1,0:T(1,128)S(1)} %get-tuple-element.21) | copy-start | bytes 36868
  52.4 195.2 %all-gather.11.cloned.1.call-start = ((), (), s32[]{:S(2)}) async-start(), calls=%async_computation.6 | async-start | bytes 15728640 | tf_op jit(solution)/shard_map/all_gather | solution.py:170
  73.2 1.2 copy-start.26
  165.5 82.1 %copy-start.10 = (bf16[1,48,3072]{2,1,0:T(8,128)(2,1)S(1)}, bf16[1,48,3072]{2,1,0:T(8,128)(2,1)}, u32[]{:S(2)}) copy-start(bf16[1,48,3072]{2,1,0:T(8,128)(2,1)} %param.19) | copy-start | bytes 884740
  171.9 90.5 %copy-start.18 = (f32[2,384]{1,0:T(2,128)}, f32[2,384]{1,0:T(2,128)S(1)}, u32[]{:S(2)}) copy-start(f32[2,384]{1,0:T(2,128)S(1)} %get-tuple-element.32) | copy-start | bytes 9220
  256.7 16.1 %all-to-all-start.1 = ((bf16[48,8,256]{2,0,1:T(8,128)(2,1)}), bf16[48,8,256]{2,0,1:T(8,128)(2,1)S(1)}, u32[]{:S(2)}, u32[]{:S(2)}) async-start(bf16[48,8,256]{2,0,1:T(8,128)(2,1)} %bitcast.142), calls=%async_computation.1 | async-start | bytes 393216 | tf_op jit(solution)/shard_map/all_to_all | solution.py:177
  262.2 108.2 %reduce-scatter.2.cloned.1.call-start = ((), (), s32[]{:S(2)}) async-start(), calls=%async_computation.7 | async-start | bytes 2654208 | tf_op jit(solution)/shard_map/reduce_scatter | solution.py:180
  263.7 11.7 %copy-start.3 = (f32[2,384,128]{1,2,0:T(8,128)}, f32[2,384,128]{1,2,0:T(8,128)S(1)}, u32[]{:S(2)}) copy-start(f32[2,384,128]{1,2,0:T(8,128)S(1)} %get-tuple-element.11) | copy-start | bytes 1179652
  263.7 11.7 %copy-start.4 = (f32[2,384,128]{1,2,0:T(8,128)}, f32[2,384,128]{1,2,0:T(8,128)S(1)}, u32[]{:S(2)}) copy-start(f32[2,384,128]{1,2,0:T(8,128)S(1)} %get-tuple-element.12) | copy-start | bytes 1179652
  272.8 2.5 copy-start.8
  275.3 2.1 copy-start.9
  277.5 1.3 copy-start.7
  279.9 1.9 copy-start.5
  281.8 13.1 %slice-start = ((s8[4718592]{0:T(1024)(128)(4,1)}), s8[524288]{0:T(1024)(128)(4,1)S(1)}, s32[]{:S(2)}) async-start(s8[4718592]{0:T(1024)(128)(4,1)} %bitcast.146), calls=%async_computation.8 | async-start | bytes 1048576
  282.8 7.8 %copy-start.22 = (f32[128]{0:T(128)S(1)}, f32[128]{0:T(128)}, u32[]{:S(2)}) copy-start(f32[128]{0:T(128)} %constant.63.clone) | copy-start | bytes 1540
  287.8 4.9 %copy-start.19 = (f32[2,384]{1,0:T(2,128)S(1)}, f32[2,384]{1,0:T(2,128)}, u32[]{:S(2)}) copy-start(f32[2,384]{1,0:T(2,128)} %copy-done.18) | copy-start | bytes 9220
  290.6 4.2 %slice-start.1 = ((s8[4718592]{0:T(1024)(128)(4,1)}), s8[4194304]{0:T(1024)(128)(4,1)S(1)}, s32[]{:S(2)}) async-start(s8[4718592]{0:T(1024)(128)(4,1)} %bitcast.146), calls=%async_computation.9 | async-start | bytes 8388608
  292.7 2.0 copy-start.12
  299.8 19.1 %copy-start.2 = (bf16[1,48,3072]{2,1,0:T(8,128)(2,1)S(1)}, bf16[1,48,3072]{2,1,0:T(8,128)(2,1)}, u32[]{:S(2)}) copy-start(bf16[1,48,3072]{2,1,0:T(8,128)(2,1)} %param.13) | copy-start | bytes 884740
  299.8 19.1 %copy-start.17 = (f32[1,3072]{1,0:T(1,128)S(1)}, f32[1,3072]{1,0:T(1,128)}, u32[]{:S(2)}) copy-start(f32[1,3072]{1,0:T(1,128)} %copy-done.16) | copy-start | bytes 36868
  318.9 51.6 %copy-start.21 = (f32[48]{0:T(128)S(1)}, f32[48]{0:T(128)}, u32[]{:S(2)}) copy-start(f32[48]{0:T(128)} %copy-done.20) | copy-start | bytes 580
  318.9 51.6 %copy-start.24 = (f32[48]{0:T(128)S(1)}, f32[48]{0:T(128)}, u32[]{:S(2)}) copy-start(f32[48]{0:T(128)} %copy-done.23) | copy-start | bytes 580
  318.9 52.8 %copy-start.11 = (bf16[1,48,3072]{2,1,0:T(8,128)(2,1)S(1)}, bf16[1,48,3072]{2,1,0:T(8,128)(2,1)}, u32[]{:S(2)}) copy-start(bf16[1,48,3072]{2,1,0:T(8,128)(2,1)} %param.19) | copy-start | bytes 884740
  (5 other events, 4.6 us)
Sparse Core Ops, SparseCore 0:
  10.2 62.9 all-gather.8
  74.7 36.1 all-gather.6
  113.7 51.8 all-gather.4
  166.9 80.6 all-gather.10
  298.5 71.9 reduce-scatter.1
where the time goes:
time: 381 us; the launch traced here: 380 us
  waiting for transfers between devices  219 us (57%)
  blocking collectives  59 us (15%)
  local copies, waits for them, and re-layouts  34.1 us (9%)
  matrix products  33.8 us (9%)
  other arithmetic  14.5 us (4%)
  between operations  14.3 us (4%)
  starting transfers between devices  5.89 us (2%)
    all_gather x1, waiting for transfers between devices, on_device(): w_all = lax.all_gather(w_heads, 'cand', axis=2, tiled=True)  75.6 us
    reduce_scatter x1, waiting for transfers between devices, on_device(): lax.psum_scatter(times_transposed(lax.slice_in_dim(d_projected, 0, rows_l...  43.6 us
    all_gather x1, waiting for transfers between devices, on_device(): gathered = lax.all_gather(modulated, 'seq', axis=0, tiled=True)  42.7 us
    all_gather x1, waiting for transfers between devices, on_device(): piece = lax.all_gather(input_weight, 'cand', axis=0, tiled=True)  34.5 us
    all_gather x1, blocking collectives, on_device(): modulation = lax.all_gather(mod_mine, 'seq', axis=1, tiled=True)[0]  31.6 us
    all_gather x1, waiting for transfers between devices, on_device(): w_heads = lax.all_gather(output_weight, 'seq', axis=0, tiled=True)  20.8 us
    all_to_all x1, blocking collectives, on_device(): lax.all_to_all(attended, 'seq', split_axis=0, concat_axis=1, tiled=True)  18.7 us
    dot_general x2, matrix products, times_transposed(): lax.dot_general(left, right, (((1,), (1,)), ((), ())), preferred_element_...  11.9 us
  transfers between devices with their start and end apart: 6, of which 5 were waited for; matrix products, arithmetic and copies ran while one was open for 11% of the time, Pallas kernels for 0%

commit v1 on v0

--- a/solution.py
+++ b/solution.py
@@ -139,7 +139,6 @@
 
 def on_device(latent, timesteps, positions, mod_weight, input_weight, output_weight, cotangent):
     width = latent.shape[2]
-    rows_local = latent.shape[1]
     groups = input_weight.shape[1]
     group_cols = groups * input_weight.shape[2]
     time_act = jax.nn.silu(time_embed(timesteps, width)).astype(jnp.bfloat16)
@@ -155,36 +154,31 @@
     shift_vec = modulation[:width]
     scale_vec = modulation[width : 2 * width]
     gate_vec = modulation[2 * width :]
+    latent_all = lax.all_gather(latent[0], "seq", axis=0, tiled=True)
+    length = latent_all.shape[0]
+    normed_all, _ = layer_norm(latent_all.astype(jnp.float32))
+    modulated = (normed_all * (1.0 + scale_vec) + shift_vec).astype(jnp.bfloat16)
+    tables = rope_tables(positions, HEAD)
+    piece = lax.all_gather(input_weight, "cand", axis=0, tiled=True).reshape(width, group_cols)
+    cot_all = lax.all_gather(cotangent[0], "seq", axis=0, tiled=True)
+    w_heads = lax.all_gather(output_weight, "cand", axis=2, tiled=True)
+    w_heads = w_heads.reshape(w_heads.shape[0] * w_heads.shape[1], width)
+    projected = jnp.dot(modulated, piece, preferred_element_type=jnp.float32)
+    attended, saved = attend(projected.reshape(length, groups, 3 * HEAD), tables)
+    mixed_part = jnp.dot(attended, w_heads, preferred_element_type=jnp.float32).astype(jnp.bfloat16)
+    mixed = lax.psum_scatter(mixed_part, "seq", scatter_dimension=0, tiled=True).astype(jnp.float32)
     latent_rows = latent[0].astype(jnp.float32)
-    normed, inverse_std = layer_norm(latent_rows)
-    modulated = (normed * (1.0 + scale_vec) + shift_vec).astype(jnp.bfloat16)
-    gathered = lax.all_gather(modulated, "seq", axis=0, tiled=True)
-    length = gathered.shape[0]
-    tables = rope_tables(positions, HEAD)
-    piece = lax.all_gather(input_weight, "cand", axis=0, tiled=True)
-    projected = jnp.dot(
-        gathered, piece.reshape(piece.shape[0], group_cols), preferred_element_type=jnp.float32
-    )
-    attended, saved = attend(projected.reshape(length, groups, 3 * HEAD), tables)
-    w_heads = lax.all_gather(output_weight, "seq", axis=0, tiled=True)
-    w_all = lax.all_gather(w_heads, "cand", axis=2, tiled=True)
-    w_all = w_all.reshape(w_all.shape[0] * w_all.shape[1], width)
-    token_heads = lax.all_to_all(attended, "seq", split_axis=0, concat_axis=1, tiled=True)
-    mixed = jnp.dot(token_heads, w_all, preferred_element_type=jnp.float32)
     block_out = (latent_rows + gate_vec * mixed).astype(jnp.bfloat16)
-    d_mixed = (cotangent[0].astype(jnp.float32) * gate_vec).astype(jnp.bfloat16)
-    d_tokens = times_transposed(d_mixed, w_all).astype(jnp.bfloat16)
-    d_attended = lax.all_to_all(d_tokens, "seq", split_axis=1, concat_axis=0, tiled=True)
+    d_mixed = (cot_all.astype(jnp.float32) * gate_vec).astype(jnp.bfloat16)
+    d_attended = times_transposed(d_mixed, w_heads).astype(jnp.bfloat16)
     d_projected = attend_back(d_attended, saved, tables)
-    w_back = lax.all_gather(input_weight, "cand", axis=0, tiled=True).reshape(width, group_cols)
     d_modulated = lax.psum_scatter(
-        times_transposed(
-            lax.slice_in_dim(d_projected, 0, rows_local * lax.axis_size("seq"), axis=0), w_back
-        ).astype(jnp.bfloat16),
+        times_transposed(d_projected, piece).astype(jnp.bfloat16),
         "seq",
         scatter_dimension=0,
         tiled=True,
     ).astype(jnp.float32)
+    normed, inverse_std = layer_norm(latent_rows)
     latent_grad = cotangent[0].astype(jnp.float32) + layer_norm_back(
         d_modulated * (1.0 + scale_vec), normed, inverse_std
     )

time: 381 us -> 381 us (level)
  waiting for transfers between devices: 219 us -> 253 us
  blocking collectives: 59 us -> 40.3 us
  matrix products: 33.8 us -> 24.5 us
  starting transfers between devices: 5.89 us -> 0.23 us
    reduce_scatter x1 -> x2, waiting for transfers between devices: 43.6 us -> 135 us  [the longest x1 70.9 us: on_device(): lax.psum_scatter(mixed_part, 'seq', scatter_dimension=0, tiled=True)]
    all_gather x4, waiting for transfers between devices: 174 us -> 115 us  [the longest x1 54 us: on_device(): cot_all = lax.all_gather(cotangent[0], 'seq', axis=0, tiled=True)]
    all_to_all x1 -> x0, blocking collectives: 18.7 us -> none  [on_device(): lax.all_to_all(attended, 'seq', split_axis=0, concat_axis=1, tiled=True)]
    all_to_all x1 -> x0, starting transfers between devices: 5.52 us -> none  [on_device(): lax.all_to_all(d_tokens, 'seq', split_axis=1, concat_axis=0, tiled=True)]
    dot_general x2, matrix products: 11.9 us -> 6.63 us  [times_transposed(): lax.dot_general(left, right, (((1,), (1,)), ((), ())), preferred_element_...]
    dot_general x3 -> x2, matrix products: 14.5 us -> 9.52 us  [the longest x1 5.5 us: on_device(): projected = jnp.dot(modulated, piece, preferred_element_type=jnp.float32)]
    unnamed x64 -> x68, local copies, waits for them, and re-layouts: 9.31 us -> 9.94 us
  transfers between devices with their start and end apart: 6 -> 6, of which waited for: 5 -> 6; matrix products, arithmetic and copies ran while one was open for 11% -> 4% of each run, Pallas kernels for 0% -> 0%
where the time goes in v1:
time: 381 us; the launch traced here: 380 us
  waiting for transfers between devices  253 us (66%)
  blocking collectives  40.3 us (11%)
  local copies, waits for them, and re-layouts  33.8 us (9%)
  matrix products  24.5 us (6%)
  between operations  14.6 us (4%)
  other arithmetic  13.7 us (4%)
    reduce_scatter x1, waiting for transfers between devices, on_device(): lax.psum_scatter(mixed_part, 'seq', scatter_dimension=0, tiled=True)  70.9 us
    reduce_scatter x1, waiting for transfers between devices, on_device(): lax.psum_scatter(times_transposed(d_projected, piece).astype(jnp.bfloat16...  64.3 us
    all_gather x1, waiting for transfers between devices, on_device(): cot_all = lax.all_gather(cotangent[0], 'seq', axis=0, tiled=True)  54 us
    all_gather x1, waiting for transfers between devices, on_device(): lax.all_gather(input_weight, 'cand', axis=0, tiled=True)  34.3 us
    all_gather x1, blocking collectives, on_device(): modulation = lax.all_gather(mod_mine, 'seq', axis=1, tiled=True)[0]  31.6 us
    all_gather x1, waiting for transfers between devices, on_device(): w_heads = lax.all_gather(output_weight, 'cand', axis=2, tiled=True)  16.7 us
    all_gather x1, waiting for transfers between devices, on_device(): latent_all = lax.all_gather(latent[0], 'seq', axis=0, tiled=True)  10.1 us
    unnamed x68, local copies, waits for them, and re-layouts  9.94 us
  transfers between devices with their start and end apart: 6, of which 6 were waited for; matrix products, arithmetic and copies ran while one was open for 4% of the time, Pallas kernels for 0%

profile of v1, /device:TPU:0, one launch (start us, length us, event | category | flops | bytes accessed | tf_op | source)
XLA Modules:
  0.0 379.9 jit_solution(7271335132875156814)
XLA Ops:
  11.9 8.7 %all-reduce = bf16[4,1152]{1,0:T(4,128)(2,1)S(1)} all-reduce(bf16[4,1152]{1,0:T(4,128)(2,1)S(1)} %convolution_convert_fusion.1), channel_id=4, replica_groups=mesh['cand'=4,'seq'=8] {'cand'}, use_global_device_ids=true, to_apply=%region_0.1.clone | all-reduce | flops 4608 | bytes 18432
  21.2 31.6 %all_gather.15 = f32[1,9216]{1,0:T(1,128)S(1)} all-gather(f32[1,1152]{1,0:T(1,128)S(1)} %dynamic-slice_convert_fusion), channel_id=1, replica_groups=mesh['cand'=4,'seq'=8] {'seq'}, dimensions={1}, use_global_device_ids=true | all-gather | bytes 41472 | tf_op jit(solution)/shard_map/all_gather | solution.py:153
  54.9 10.1 %all-gather.11.cloned.1.call-done = bf16[1,384,3072]{2,1,0:T(8,128)(2,1)} async-done(((bf16[1,48,3072]{2,1,0:T(8,128)(2,1)}), bf16[1,384,3072]{2,1,0:T(8,128)(2,1)}) %all-gather.11.cloned.1.call-update) | async-done | bytes 2359312 | tf_op jit(solution)/shard_map/all_gather | solution.py:157
  65.0 2.2 convert_reduce_fusion
  68.1 16.7 %all-gather.9.cloned.1.call-done = bf16[2,128,3072]{2,1,0:T(8,128)(2,1)} async-done(((bf16[2,128,768]{2,1,0:T(8,128)(2,1)}), bf16[2,128,3072]{2,1,0:T(8,128)(2,1)}) %all-gather.9.cloned.1.call-update) | async-done | bytes 1572880 | tf_op jit(solution)/shard_map/all_gather | solution.py:164
  84.8 54.0 %all-gather.13.cloned.1.call-done = bf16[1,384,3072]{2,1,0:T(8,128)(2,1)} async-done(((bf16[1,48,3072]{2,1,0:T(8,128)(2,1)}), bf16[1,384,3072]{2,1,0:T(8,128)(2,1)}) %all-gather.13.cloned.1.call-update) | async-done | bytes 2359312 | tf_op jit(solution)/shard_map/all_gather | solution.py:163
  138.9 3.1 fusion.24
  142.0 34.3 %all-gather.7.cloned.1.call-done = bf16[3072,2,384]{2,1,0:T(2,128)(2,1)} async-done(((bf16[768,2,384]{2,1,0:T(2,128)(2,1)}), bf16[3072,2,384]{2,1,0:T(2,128)(2,1)}) %all-gather.7.cloned.1.call-update) | async-done | bytes 4718608 | tf_op jit(solution)/shard_map/all_gather | solution.py:162
  176.3 5.3 %copy.73 = bf16[384,8,2,384]{3,1,2,0:T(8,128)(2,1)} copy(bf16[384,8,2,384]{3,2,1,0:T(2,128)(2,1)} %bitcast.164) | data formatting | bytes 9437184
  181.5 6.7 %copy.42 = bf16[3072,768]{0,1:T(8,128)(2,1)} copy(bf16[3072,768]{1,0:T(8,128)(2,1)} %bitcast.160) | data formatting | bytes 9437184 | tf_op jit(solution)/shard_map/reshape | solution.py:162
  188.3 5.5 %fusion.19 = f32[3,2,384,128]{2,3,0,1:T(8,128)S(1)} fusion(bf16[2,3,128,3072]{3,2,1,0:T(8,128)(2,1)} %bitcast.165, bf16[1,384,3072]{2,1,0:T(8,128)(2,1)} %all-gather.11.cloned.1.call-done, f32[3072]{0:T(1024)S(1)} %bitcast.175, f32[3072]{0:T(1024)S(1)} %bitcast.170, f32[384]{0:T(512)S(1)} %add_rsqrt_fusion.2, f32[384]{0:T(512)S(1)} %broadcast_multiply_fusion.9), kind=kOutput, calls=%fused_computation.27 | convolution fusion | flops 1819017216 | bytes 8285184 | tf_op jit(solution)/shard_map/dot_general | solution.py:166
  194.9 1.1 copy.44
  195.9 1.1 copy.46
  197.0 2.2 gather_fusion
  199.2 2.9 gather_fusion.1
  202.1 2.5 fusion.58
  204.5 1.6 fusion.46
  206.1 2.1 multiply_reduce_fusion
  208.2 2.0 fusion.28
  211.5 1.1 broadcast_multiply_fusion
  212.6 1.1 copy.58
  213.7 2.9 gather_fusion.3
  216.6 2.1 copy.55
  218.7 2.9 gather_fusion.2
  221.6 2.0 multiply_reduce_fusion.2
  224.4 0.9 slice-done.1
  225.3 3.5 convolution_convert_fusion
  228.9 4.0 %bitcast_convert_fusion = bf16[384,3072]{1,0:T(8,128)(2,1)} fusion(bf16[2,128,3072]{2,1,0:T(8,128)(2,1)} %all-gather.9.cloned.1.call-done, f32[2,384,384]{1,2,0:T(8,128)S(1)} %get-tuple-element.31, f32[3,2,384,128]{2,3,0,1:T(8,128)} %copy-done.10), kind=kOutput, calls=%fused_computation.15 | convolution fusion | flops 681050112 | bytes 5308416 | tf_op jit(solution)/shard_map/dot_general | solution.py:168
  234.3 64.3 %reduce-scatter.5.cloned.1.call-done = bf16[48,3072]{1,0:T(8,128)(2,1)} async-done(((bf16[384,3072]{1,0:T(8,128)(2,1)}), bf16[48,3072]{1,0:T(8,128)(2,1)}) %reduce-scatter.5.cloned.1.call-update) | async-done | bytes 294928 | tf_op jit(solution)/shard_map/reduce_scatter | solution.py:175
  298.6 1.2 fusion.42
  299.8 70.9 %reduce-scatter.3.cloned.1.call-done = bf16[48,3072]{1,0:T(8,128)(2,1)} async-done(((bf16[384,3072]{1,0:T(8,128)(2,1)}), bf16[48,3072]{1,0:T(8,128)(2,1)}) %reduce-scatter.3.cloned.1.call-update) | async-done | bytes 294928 | tf_op jit(solution)/shard_map/reduce_scatter | solution.py:169
  370.8 2.3 fusion.39
  (113 shorter events, 12.6 us)
Async XLA Ops:
  7.2 4.3 %copy-start = (bf16[768,1152]{1,0:T(8,128)(2,1)S(1)}, bf16[768,1152]{1,0:T(8,128)(2,1)}, u32[]{:S(2)}) copy-start(bf16[768,1152]{1,0:T(8,128)(2,1)} %param.16) | copy-start | bytes 5308420
  7.2 2.9 copy-start.30
  7.2 2.9 copy-start.29
  7.2 3.5 copy-start.27
  7.2 57.8 %all-gather.11.cloned.1.call-start = ((), (), s32[]{:S(2)}) async-start(), calls=%async_computation.6 | async-start | bytes 2654208 | tf_op jit(solution)/shard_map/all_gather | solution.py:157
  7.9 76.9 %all-gather.9.cloned.1.call-start = ((), (), s32[]{:S(2)}) async-start(), calls=%async_computation.3 | async-start | bytes 1966080 | tf_op jit(solution)/shard_map/all_gather | solution.py:164
  8.7 130.2 %all-gather.13.cloned.1.call-start = ((), (), s32[]{:S(2)}) async-start(), calls=%async_computation.7 | async-start | bytes 2654208 | tf_op jit(solution)/shard_map/all_gather | solution.py:163
  9.4 43.4 %copy-start.28 = (s32[128]{0:T(128)S(1)}, s32[128]{0:T(128)}, u32[]{:S(2)}) copy-start(s32[128]{0:T(128)} %constant.73) | copy-start | bytes 1540
  9.4 166.8 %all-gather.7.cloned.1.call-start = ((), (), s32[]{:S(2)}) async-start(), calls=%async_computation.2 | async-start | bytes 5898240 | tf_op jit(solution)/shard_map/all_gather | solution.py:162
  10.0 288.6 %reduce-scatter.5.cloned.1.call-start = ((), (), s32[]{:S(2)}) async-start(), calls=%async_computation.5 | async-start | bytes 2654208 | tf_op jit(solution)/shard_map/reduce_scatter | solution.py:175
  54.9 84.0 %copy-start.22 = (f32[1,3072]{1,0:T(1,128)}, f32[1,3072]{1,0:T(1,128)S(1)}, u32[]{:S(2)}) copy-start(f32[1,3072]{1,0:T(1,128)S(1)} %get-tuple-element.23) | copy-start | bytes 36868
  65.0 2.4 copy-start.5
  142.0 60.1 %copy-start.18 = (bf16[384,256]{0,1:T(8,128)(2,1)}, bf16[384,256]{0,1:T(8,128)(2,1)S(1)}, u32[]{:S(2)}) copy-start(bf16[384,256]{0,1:T(8,128)(2,1)S(1)} %fusion.24) | copy-start | bytes 589828
  193.9 2.1 copy-start.24
  194.9 11.2 %copy-start.3 = (f32[2,384,128]{1,2,0:T(8,128)}, f32[2,384,128]{1,2,0:T(8,128)S(1)}, u32[]{:S(2)}) copy-start(f32[2,384,128]{1,2,0:T(8,128)S(1)} %get-tuple-element.12) | copy-start | bytes 1179652
  194.9 13.3 %copy-start.1 = (f32[2,384,128]{1,2,0:T(8,128)}, f32[2,384,128]{1,2,0:T(8,128)S(1)}, u32[]{:S(2)}) copy-start(f32[2,384,128]{1,2,0:T(8,128)S(1)} %get-tuple-element.11) | copy-start | bytes 1179652
  202.1 2.5 copy-start.15
  212.6 9.0 %copy-start.26 = (f32[128]{0:T(128)S(1)}, f32[128]{0:T(128)}, u32[]{:S(2)}) copy-start(f32[128]{0:T(128)} %constant.67.clone) | copy-start | bytes 1540
  212.6 11.8 %slice-start = ((s8[4718592]{0:T(1024)(128)(4,1)}), s8[524288]{0:T(1024)(128)(4,1)S(1)}, s32[]{:S(2)}) async-start(s8[4718592]{0:T(1024)(128)(4,1)} %bitcast.161), calls=%async_computation.8 | async-start | bytes 1048576
  218.6 5.0 %copy-start.25 = (f32[2,384]{1,0:T(2,128)S(1)}, f32[2,384]{1,0:T(2,128)}, u32[]{:S(2)}) copy-start(f32[2,384]{1,0:T(2,128)} %copy-done.24) | copy-start | bytes 9220
  221.5 2.2 copy-start.2
  221.5 2.2 copy-start.4
  221.5 2.2 copy-start.8
  221.5 2.2 copy-start.11
  221.5 2.3 copy-start.12
  221.5 2.4 copy-start.13
  221.5 2.4 copy-start.14
  221.6 2.7 copy-start.17
  221.6 3.8 slice-start.1
  228.9 141.9 %reduce-scatter.3.cloned.1.call-start = ((), (), s32[]{:S(2)}) async-start(), calls=%async_computation.4 | async-start | bytes 2654208 | tf_op jit(solution)/shard_map/reduce_scatter | solution.py:169
  232.9 137.8 %copy-start.16 = (bf16[1,48,3072]{2,1,0:T(8,128)(2,1)S(1)}, bf16[1,48,3072]{2,1,0:T(8,128)(2,1)}, u32[]{:S(2)}) copy-start(bf16[1,48,3072]{2,1,0:T(8,128)(2,1)} %param.19) | copy-start | bytes 884740
  232.9 137.8 %copy-start.23 = (f32[1,3072]{1,0:T(1,128)S(1)}, f32[1,3072]{1,0:T(1,128)}, u32[]{:S(2)}) copy-start(f32[1,3072]{1,0:T(1,128)} %copy-done.22) | copy-start | bytes 36868
  (7 other events, 8.6 us)
Sparse Core Ops, SparseCore 0:
  10.2 54.7 all-gather.10
  66.5 18.2 all-gather.8
  87.0 51.8 all-gather.12
  140.3 35.9 all-gather.6
  229.0 69.5 reduce-scatter.4
  301.9 68.7 reduce-scatter.2

commit v2 on v1

v2 whole, which is shorter than its diff:
```python
import functools

import jax
import jax.numpy as jnp
import numpy as np
from jax import lax
from jax.experimental import pallas as pl
from jax.experimental.pallas import tpu as pltpu
from jax.sharding import PartitionSpec as P

HEAD = 128
CHUNKS = 4
MESH = pl.DeviceIdType.MESH


epsilon = 1e-06


def time_embed(timesteps, feature_width):
    half_size = feature_width // 2
    freq_rate = jnp.exp(-jnp.log(10000.0) * jnp.arange(half_size, dtype=jnp.float32) / half_size)
    angles = timesteps.astype(jnp.float32)[:, None] * freq_rate[None, :]
    return jnp.concatenate([jnp.cos(angles), jnp.sin(angles)], axis=1)


def rope_tables(positions, head_size):
    first_size = head_size // 8
    other_size = (head_size - first_size) // 2
    pieces = []
    swapped = []
    sign_vec = []
    offset = 0
    for axis_id, width_part in enumerate((first_size, other_size, other_size)):
        half_size = width_part // 2
        freq_rate = jnp.exp(
            -jnp.log(256.0) * 2.0 * jnp.arange(half_size, dtype=jnp.float32) / width_part
        )
        angle_part = positions[axis_id].astype(jnp.float32)[:, None] * freq_rate[None, :]
        pieces.append(angle_part)
        pieces.append(angle_part)
        swapped += list(range(offset + half_size, offset + width_part)) + list(
            range(offset, offset + half_size)
        )
        sign_vec += [-1.0] * half_size + [1.0] * half_size
        offset += width_part
    angles = jnp.concatenate(pieces, axis=1)
    return (
        jnp.cos(angles),
        jnp.sin(angles),
        np.array(swapped, np.int32),
        np.array(sign_vec, np.float32),
    )


def swap_pairs(values):
    lane = lax.broadcasted_iota(jnp.int32, values.shape, 1)
    small = HEAD // 8
    large = (HEAD - small) // 2
    near = jnp.where(
        lane < small // 2,
        pltpu.roll(values, HEAD - small // 2, 1),
        pltpu.roll(values, small // 2, 1),
    )
    upper = ((lane >= small) & (lane < small + large // 2)) | (
        (lane >= small + large) & (lane < small + large + large // 2)
    )
    far = jnp.where(
        upper, pltpu.roll(values, HEAD - large // 2, 1), pltpu.roll(values, large // 2, 1)
    )
    return jnp.where(lane < small, near, far)


def dot_nt(left, right):
    return lax.dot_general(left, right, (((1,), (1,)), ((), ())), preferred_element_type=jnp.float32)


def dot_tn(left, right):
    return lax.dot_general(left, right, (((0,), (0,)), ((), ())), preferred_element_type=jnp.float32)


def inverse_rms(values):
    return lax.rsqrt(jnp.mean(values * values, -1, keepdims=True) + epsilon)


def layer_norm(values):
    centred = values - jnp.mean(values, -1, keepdims=True)
    inverse_std = lax.rsqrt(jnp.mean(centred * centred, -1, keepdims=True) + epsilon)
    return (centred * inverse_std, inverse_std)


def step_kernel(
    nc, ns,
    act_ref, cos_ref, sin_ref, mod_w_ref, latent_ref, cot_ref, w_in_ref, w_out_ref,
    block_ref, grad_ref,
    part, part_in, mine, mod_all, vecs,
    lat_all, cot_all, w_in_all, w_out_all, x_all, proj, q_all, k_all, v_all, probs, att, d_att,
    d_proj, mix_out, mix_in, dm_out, dm_in,
    own_sem, lat_s, lat_r, cot_s, cot_r, wi_s, wi_r, wo_s, wo_r, m1_s, m1_r, m2_s, m2_r,
    mx_s, mx_r, dm_s, dm_r,
):
    me_c = lax.axis_index("cand")
    me_s = lax.axis_index("seq")
    rows, width = latent_ref.shape
    length = rows * ns
    slab = w_in_ref.shape[0]
    groups = q_all.shape[0]
    cols = mod_w_ref.shape[1]
    piece = w_out_ref.shape[1]
    chunk = width // CHUNKS
    half = nc // 2
    mate = me_c + 1 - 2 * lax.rem(me_c, 2)
    score_scale = HEAD ** (-0.5)

    def seq_peer(k):
        return lax.rem(me_s + k, ns)

    def rows_of(index, size):
        return pl.ds(pl.multiple_of(index * size, size), size)

    def remote(src, dst, send, recv, cand, seq):
        copy = pltpu.make_async_remote_copy(
            src_ref=src, dst_ref=dst, send_sem=send, recv_sem=recv,
            device_id=(cand, seq), device_id_type=MESH,
        )
        copy.start()
        return copy

    barrier = pltpu.get_barrier_semaphore()
    for k in range(1, nc):
        pl.semaphore_signal(
            barrier, inc=1, device_id=(lax.rem(me_c + k, nc), me_s), device_id_type=MESH
        )
    for k in range(1, ns):
        pl.semaphore_signal(barrier, inc=1, device_id=(me_c, seq_peer(k)), device_id_type=MESH)

    own = [
        pltpu.make_async_copy(latent_ref, lat_all.at[rows_of(me_s, rows)], own_sem.at[0]),
        pltpu.make_async_copy(cot_ref, cot_all.at[rows_of(me_s, rows)], own_sem.at[1]),
        pltpu.make_async_copy(w_in_ref, w_in_all.at[rows_of(me_c, slab)], own_sem.at[2]),
        pltpu.make_async_copy(w_out_ref, w_out_all.at[me_c], own_sem.at[3]),
    ]
    for copy in own:
        copy.start()
    product = jnp.dot(act_ref[...], mod_w_ref[...], preferred_element_type=jnp.float32)
    for c in range(nc):
        part[c] = product[8 * c : 8 * c + 8]
    pl.semaphore_wait(barrier, nc - 1 + ns - 1)

    lat = [
        remote(latent_ref, lat_all.at[rows_of(me_s, rows)], lat_s.at[k], lat_r.at[k], me_c, seq_peer(k))
        for k in range(1, ns)
    ]
    m1 = []
    for k in range(1, nc):
        peer = lax.rem(me_c + k, nc)
        m1.append(remote(part.at[peer], part_in.at[me_c], m1_s.at[k], m1_r.at[k], peer, me_s))

    def cand_gather(src, place, send, recv):
        first = [remote(src, place(me_c), send.at[0], recv.at[0], mate, me_s)]
        for j in range(1, half):
            peer = lax.rem(me_c + 2 * j, nc)
            first.append(remote(src, place(me_c), send.at[j], recv.at[j], peer, me_s))
        return first

    def cand_forward(first, place, send, recv):
        second = []
        for j in range(1, half):
            first[j].wait_recv()
            held = place(lax.rem(me_c - 2 * j + nc, nc))
            second.append(remote(held, held, send.at[half + j], recv.at[half + j], mate, me_s))
        return second

    def in_place(index):
        return w_in_all.at[rows_of(index, slab)]

    def out_place(index):
        return w_out_all.at[index]

    w_in = cand_gather(w_in_ref, in_place, wi_s, wi_r)
    w_out = cand_gather(w_out_ref, out_place, wo_s, wo_r)

    for copy in m1:
        copy.wait_recv()
    total = part[me_c]
    for k in range(1, nc):
        total = total + part_in[lax.rem(me_c - k + nc, nc)]
    mine[...] = total
    mod_all[me_s] = total
    m2 = [
        remote(mine, mod_all.at[me_s], m2_s.at[k], m2_r.at[k], me_c, seq_peer(k))
        for k in range(1, ns)
    ]
    cot = [
        remote(cot_ref, cot_all.at[rows_of(me_s, rows)], cot_s.at[k], cot_r.at[k], me_c, seq_peer(k))
        for k in range(1, ns)
    ]
    for copy in lat + m2:
        copy.wait_recv()
    own[0].wait()
    for s in range(ns):
        at = s * cols
        while at < (s + 1) * cols:
            kind = at // width
            stop = min((s + 1) * cols, (kind + 1) * width)
            vecs[kind, :, at - kind * width : stop - kind * width] = mod_all[
                s, :, at - s * cols : stop - s * cols
            ]
            at = stop

    def norm_rows(index, _):
        at = rows_of(index, 16)
        normed, _inverse = layer_norm(lat_all[at].astype(jnp.float32))
        x_all[at] = (normed * (1.0 + vecs[1, 0:1]) + vecs[0, 0:1]).astype(jnp.bfloat16)
        return 0

    lax.fori_loop(0, length // 16, norm_rows, 0)
    w_in_second = cand_forward(w_in, in_place, wi_s, wi_r)
    w_in[0].wait_recv()
    own[2].wait()
    for copy in w_in_second:
        copy.wait_recv()
    w_out_second = cand_forward(w_out, out_place, wo_s, wo_r)

    tile = 3 * HEAD

    def project(index, _):
        at = pl.ds(pl.multiple_of(index * tile, tile), tile)
        proj[index] = jnp.dot(x_all[...], w_in_all[:, at], preferred_element_type=jnp.float32)
        return 0

    lax.fori_loop(0, groups, project, 0)

    def head_forward(h, _):
        query = proj[h, :, 0:HEAD]
        key = proj[h, :, HEAD : 2 * HEAD]
        query_n = query * inverse_rms(query)
        key_n = key * inverse_rms(key)
        q_rot = (query_n * cos_ref[...] + swap_pairs(query_n) * sin_ref[...]).astype(jnp.bfloat16)
        k_rot = (key_n * cos_ref[...] + swap_pairs(key_n) * sin_ref[...]).astype(jnp.bfloat16)
        values = proj[h, :, 2 * HEAD :].astype(jnp.bfloat16)
        q_all[h] = q_rot
        k_all[h] = k_rot
        v_all[h] = values
        weights = jnp.exp(dot_nt(q_rot, k_rot) * score_scale - HEAD**0.5)
        share = weights * (1.0 / jnp.sum(weights, -1, keepdims=True))
        probs[h] = share
        att[h] = jnp.dot(
            share.astype(jnp.bfloat16), values, preferred_element_type=jnp.float32
        ).astype(jnp.bfloat16)
        return 0

    lax.fori_loop(0, groups, head_forward, 0)

    own[3].wait()
    w_out[0].wait_recv()
    for copy in w_out_second:
        copy.wait_recv()

    def scatter(out, into, send, recv, j):
        copies = []
        for k in range(1, ns):
            peer = seq_peer(k)
            copies.append(
                remote(out.at[j, rows_of(peer, rows)], into.at[j, me_s], send.at[j, k], recv.at[j, k], me_c, peer)
            )
        return copies

    mixed = []
    per_chunk = chunk // piece
    for j in range(CHUNKS):
        for i in range(per_chunk):
            c = j * per_chunk + i
            block = jnp.zeros((length, piece), jnp.float32)
            for h in range(groups):
                block = block + jnp.dot(
                    att[h], w_out_all[c, h * HEAD : (h + 1) * HEAD], preferred_element_type=jnp.float32
                )
            mix_out[j, :, i * piece : (i + 1) * piece] = block.astype(jnp.bfloat16)
        mixed.append(scatter(mix_out, mix_in, mx_s, mx_r, j))

    for copy in cot:
        copy.wait_recv()
    own[1].wait()

    def gate_rows(index, _):
        at = rows_of(index, 16)
        x_all[at] = (cot_all[at].astype(jnp.float32) * vecs[2, 0:1]).astype(jnp.bfloat16)
        return 0

    lax.fori_loop(0, length // 16, gate_rows, 0)
    for h in range(groups):
        block = jnp.zeros((length, HEAD), jnp.float32)
        for c in range(nc):
            block = block + dot_nt(
                x_all[:, c * piece : (c + 1) * piece], w_out_all[c, h * HEAD : (h + 1) * HEAD]
            )
        d_att[h] = block.astype(jnp.bfloat16)

    def back_norm(d_rot, raw):
        inverse = inverse_rms(raw)
        normed = raw * inverse
        d_normed = d_rot * cos_ref[...] - swap_pairs(d_rot) * sin_ref[...]
        return inverse * (d_normed - normed * jnp.mean(d_normed * normed, -1, keepdims=True))

    def head_backward(h, _):
        d_heads = d_att[h]
        share = probs[h]
        d_values = dot_tn(share.astype(jnp.bfloat16), d_heads)
        d_probs = dot_nt(d_heads, v_all[h])
        d_scores = (share * (d_probs - jnp.sum(share * d_probs, -1, keepdims=True))).astype(
            jnp.bfloat16
        )
        d_qrot = jnp.dot(d_scores, k_all[h], preferred_element_type=jnp.float32) * score_scale
        d_krot = dot_tn(d_scores, q_all[h]) * score_scale
        d_query = back_norm(d_qrot, proj[h, :, 0:HEAD])
        d_key = back_norm(d_krot, proj[h, :, HEAD : 2 * HEAD])
        d_proj[h, :, 0:HEAD] = d_query.astype(jnp.bfloat16)
        d_proj[h, :, HEAD : 2 * HEAD] = d_key.astype(jnp.bfloat16)
        d_proj[h, :, 2 * HEAD :] = d_values.astype(jnp.bfloat16)
        return 0

    lax.fori_loop(0, groups, head_backward, 0)

    d_mod = []
    for j in range(CHUNKS):
        block = jnp.zeros((length, chunk), jnp.float32)
        for h in range(groups):
            block = block + dot_nt(
                d_proj[h], w_in_all[j * chunk : (j + 1) * chunk, h * tile : (h + 1) * tile]
            )
        dm_out[j] = block.astype(jnp.bfloat16)
        d_mod.append(scatter(dm_out, dm_in, dm_s, dm_r, j))

    def summed(out, into, j, at):
        start = pl.multiple_of(me_s * rows, rows) + at
        result = out[j, pl.ds(pl.multiple_of(start, 16), 16)].astype(jnp.float32)
        for k in range(1, ns):
            result = result + into[j, lax.rem(me_s + k, ns), at : at + 16].astype(jnp.float32)
        return result

    for j in range(CHUNKS):
        for copy in mixed[j]:
            copy.wait_recv()
    for at in range(0, rows, 16):
        for j in range(CHUNKS):
            part_cols = slice(j * chunk, (j + 1) * chunk)
            own_rows = pl.ds(pl.multiple_of(me_s * rows + at, 16), 16)
            block_ref[at : at + 16, part_cols] = (
                lat_all[own_rows, part_cols].astype(jnp.float32)
                + vecs[2, 0:1, part_cols] * summed(mix_out, mix_in, j, at)
            ).astype(jnp.bfloat16)

    for j in range(CHUNKS):
        for copy in d_mod[j]:
            copy.wait_recv()
    for at in range(0, rows, 16):
        own_rows = pl.ds(pl.multiple_of(me_s * rows + at, 16), 16)
        normed, inverse_std = layer_norm(lat_all[own_rows].astype(jnp.float32))
        d_normed = jnp.concatenate(
            [summed(dm_out, dm_in, j, at) for j in range(CHUNKS)], axis=1
        ) * (1.0 + vecs[1, 0:1])
        grad_ref[at : at + 16] = cot_all[own_rows].astype(jnp.float32) + inverse_std * (
            d_normed
            - jnp.mean(d_normed, -1, keepdims=True)
            - normed * jnp.mean(d_normed * normed, -1, keepdims=True)
        )

    for copy in lat + m1 + m2 + cot + w_in + w_out + w_in_second + w_out_second:
        copy.wait_send()
    for j in range(CHUNKS):
        for copy in mixed[j] + d_mod[j]:
            copy.wait_send()


def on_device(latent, timesteps, positions, mod_weight, input_weight, output_weight, cotangent):
    nc = lax.axis_size("cand")
    ns = lax.axis_size("seq")
    rows, width = latent.shape[1:]
    length = rows * ns
    slab = input_weight.shape[0]
    groups = input_weight.shape[1]
    cols = mod_weight.shape[1]
    piece = output_weight.shape[2]
    chunk = width // CHUNKS
    time_act = jax.nn.silu(time_embed(timesteps, width)).astype(jnp.bfloat16)
    act_rows = lax.dynamic_slice_in_dim(time_act, lax.axis_index("cand") * slab, slab, 1)
    act_rows = jnp.repeat(act_rows, 8, axis=0)
    cos_tab, sin_tab, _swapped, sign_vec = rope_tables(positions, HEAD)
    vmem = pl.BlockSpec(memory_space=pltpu.VMEM)
    anywhere = pl.BlockSpec(memory_space=pl.ANY)
    f32, bf16 = jnp.float32, jnp.bfloat16
    dma = pltpu.SemaphoreType.DMA
    block_out, latent_grad = pl.pallas_call(
        functools.partial(step_kernel, nc, ns),
        out_shape=(
            jax.ShapeDtypeStruct((rows, width), bf16),
            jax.ShapeDtypeStruct((rows, width), f32),
        ),
        in_specs=[vmem] * 4 + [anywhere] * 4,
        out_specs=(vmem, vmem),
        scratch_shapes=[
            pltpu.VMEM((nc, 8, cols), f32),
            pltpu.VMEM((nc, 8, cols), f32),
            pltpu.VMEM((8, cols), f32),
            pltpu.VMEM((ns, 8, cols), f32),
            pltpu.VMEM((3, 8, width), f32),
            pltpu.VMEM((length, width), bf16),
            pltpu.VMEM((length, width), bf16),
            pltpu.VMEM((slab * nc, groups * 3 * HEAD), bf16),
            pltpu.VMEM((nc, groups * HEAD, piece), bf16),
            pltpu.VMEM((length, width), bf16),
            pltpu.VMEM((groups, length, 3 * HEAD), f32),
            pltpu.VMEM((groups, length, HEAD), bf16),
            pltpu.VMEM((groups, length, HEAD), bf16),
            pltpu.VMEM((groups, length, HEAD), bf16),
            pltpu.VMEM((groups, length, length), f32),
            pltpu.VMEM((groups, length, HEAD), bf16),
            pltpu.VMEM((groups, length, HEAD), bf16),
            pltpu.VMEM((groups, length, 3 * HEAD), bf16),
            pltpu.VMEM((CHUNKS, length, chunk), bf16),
            pltpu.VMEM((CHUNKS, ns, rows, chunk), bf16),
            pltpu.VMEM((CHUNKS, length, chunk), bf16),
            pltpu.VMEM((CHUNKS, ns, rows, chunk), bf16),
            dma((4,)),
            dma((ns,)), dma((ns,)), dma((ns,)), dma((ns,)),
            dma((nc,)), dma((nc,)), dma((nc,)), dma((nc,)),
            dma((nc,)), dma((nc,)), dma((ns,)), dma((ns,)),
            dma((CHUNKS, ns)), dma((CHUNKS, ns)), dma((CHUNKS, ns)), dma((CHUNKS, ns)),
        ],
        compiler_params=pltpu.CompilerParams(
            collective_id=0, has_side_effects=True, vmem_limit_bytes=66000000
        ),
    )(
        act_rows, cos_tab, sin_tab * sign_vec, mod_weight, latent[0], cotangent[0],
        input_weight.reshape(slab, groups * 3 * HEAD),
        output_weight.reshape(groups * HEAD, piece),
    )
    return (block_out[None], latent_grad[None])


def solution(mesh):
    placed = (
        P("cand", "seq", None),
        P(),
        P(),
        P("cand", "seq"),
        P("cand", "seq", None),
        P("seq", None, "cand"),
        P("cand", "seq", None),
    )
    return jax.shard_map(
        on_device,
        mesh=mesh,
        in_specs=placed,
        out_specs=(P("cand", "seq", None), P("cand", "seq", None)),
        check_vma=False,
    )
```

time: 381 us -> 229 us (0.60)
  waiting for transfers between devices: 253 us -> 0 us
  Pallas kernels: 0 us -> 218 us
  blocking collectives: 40.3 us -> 0 us
  local copies, waits for them, and re-layouts: 33.8 us -> 5.82 us
  matrix products: 24.5 us -> 0 us
  between operations: 14.6 us -> 0.71 us
  other arithmetic: 13.7 us -> 3.54 us
    pallas_call x0 -> x1, Pallas kernels: none -> 218 us  [on_device(): pl.pallas_call(functools.partial(step_kernel, nc, ns), out_shape=(jax.Sha...]
    reduce_scatter x2 -> x0, waiting for transfers between devices: 135 us -> none  [the longest x1 70.9 us: on_device(): lax.psum_scatter(mixed_part, 'seq', scatter_dimension=0, tiled=True)]
    all_gather x4 -> x0, waiting for transfers between devices: 115 us -> none  [the longest x1 54 us: on_device(): cot_all = lax.all_gather(cotangent[0], 'seq', axis=0, tiled=True)]
    all_gather x1 -> x0, blocking collectives: 31.6 us -> none  [on_device(): modulation = lax.all_gather(mod_mine, 'seq', axis=1, tiled=True)[0]]
    dot_general x9 -> x0, matrix products: 22.4 us -> none  [the longest x2 6.63 us: times_transposed(): lax.dot_general(left, right, (((1,), (1,)), ((), ())), preferred_element_...]
    gather x4 -> x0, local copies, waits for them, and re-layouts: 10.8 us -> none  [the longest x2 5.72 us: unrotate(): return values * cos_tab - (values * sin_tab)[..., swapped] * sign_vec]
    unnamed x1 -> x0, blocking collectives: 8.69 us -> none
    reduce_sum x7 -> x0, other arithmetic: 6.71 us -> none  [the longest x2 2.35 us: layer_norm(): centred = values - jnp.mean(values, -1, keepdims=True)]
  transfers between devices with their start and end apart: 6 -> 0, of which waited for: 6 -> 0; matrix products, arithmetic and copies ran while one was open for 4% -> 0% of each run, Pallas kernels for 0% -> 0%
where the time goes in v2:
time: 229 us; the launch traced here: 228 us
  Pallas kernels  218 us (95%)
  local copies, waits for them, and re-layouts  5.82 us (3%)
  other arithmetic  3.54 us (2%)
    pallas_call x1, Pallas kernels, on_device(): pl.pallas_call(functools.partial(step_kernel, nc, ns), out_shape=(jax.Sha...  218 us
    unnamed x7, local copies, waits for them, and re-layouts  4.87 us

profile of v2, /device:TPU:0, one launch (start us, length us, event | category | flops | bytes accessed | tf_op | source)
XLA Modules:
  0.0 228.4 jit_solution(8843747106088927245)
XLA Ops:
  0.6 0.0 copy-start.1
  0.6 0.7 convert_element_type.36
  1.3 0.8 convert_reduce_fusion
  2.2 0.3 multiply_cosine_fusion
  2.5 0.6 broadcast_bitcast_fusion.act_ref
  3.1 0.1 broadcast_multiply_fusion.2
  3.2 0.0 copy-start
  3.2 0.2 broadcast_multiply_fusion
  3.4 0.3 concatenate.7
  3.8 0.0 copy-done.1
  3.8 1.4 sine_multiply_fusion
  5.2 0.0 copy-done
  5.2 1.2 copy.10
  6.4 218.3 %shard_map.95 = (bf16[48,3072]{1,0:T(8,128)(2,1)}, f32[48,3072]{1,0:T(8,128)}) custom-call(bf16[32,768]{1,0:T(8,128)(2,1)} %broadcast_bitcast_fusion.act_ref, f32[384,128]{1,0:T(8,128)} %get-tuple-element.10.cos_ref, f32[384,128]{1,0:T(8,128)} %get-tuple-element.9.sin_ref, bf16[768,1152]{1,0:T(8,128)(2,1)} %mod_w_ref.1, bf16[48,3072]{1,0:T(8,128)(2,1)} %bitcast.13, ...), custom_call_target="tpu_custom_call" | custom-call | tf_op jit(solution)/shard_map/pallas_call | solution.py:393
  224.8 1.7 copy.13
  226.5 1.9 copy.14
  (4 shorter events, 0.1 us)
Async XLA Ops:
  0.6 3.1 %copy-start.1 = (f32[128]{0:T(128)S(1)}, f32[128]{0:T(128)}, u32[]{:S(2)}) copy-start(f32[128]{0:T(128)} %constant.31.clone) | copy-start | bytes 1540
  3.2 2.0 copy-start

commit v3 on v2

--- a/solution.py
+++ b/solution.py
@@ -94,9 +94,9 @@
     block_ref, grad_ref,
     part, part_in, mine, mod_all, vecs,
     lat_all, cot_all, w_in_all, w_out_all, x_all, proj, q_all, k_all, v_all, probs, att, d_att,
-    d_proj, mix_out, mix_in, dm_out, dm_in,
+    d_proj, mix_out, mix_near, mix_sum, mix_in, dm_out, dm_near, dm_sum, dm_in,
     own_sem, lat_s, lat_r, cot_s, cot_r, wi_s, wi_r, wo_s, wo_r, m1_s, m1_r, m2_s, m2_r,
-    mx_s, mx_r, dm_s, dm_r,
+    mxn_s, mxn_r, mx_s, mx_r, dmn_s, dmn_r, dm_s, dm_r,
 ):
     me_c = lax.axis_index("cand")
     me_s = lax.axis_index("seq")
@@ -109,10 +109,16 @@
     chunk = width // CHUNKS
     half = nc // 2
     mate = me_c + 1 - 2 * lax.rem(me_c, 2)
+    far = ns // 2
+    me_y, me_z = lax.rem(me_s, 2), lax.div(me_s, 2)
+    near = me_s + 1 - 2 * me_y
     score_scale = HEAD ** (-0.5)
 
     def seq_peer(k):
         return lax.rem(me_s + k, ns)
+
+    def place(index):
+        return lax.rem(index, 2) * far + lax.div(index, 2)
 
     def rows_of(index, size):
         return pl.ds(pl.multiple_of(index * size, size), size)
@@ -134,8 +140,8 @@
         pl.semaphore_signal(barrier, inc=1, device_id=(me_c, seq_peer(k)), device_id_type=MESH)
 
     own = [
-        pltpu.make_async_copy(latent_ref, lat_all.at[rows_of(me_s, rows)], own_sem.at[0]),
-        pltpu.make_async_copy(cot_ref, cot_all.at[rows_of(me_s, rows)], own_sem.at[1]),
+        pltpu.make_async_copy(latent_ref, lat_all.at[rows_of(place(me_s), rows)], own_sem.at[0]),
+        pltpu.make_async_copy(cot_ref, cot_all.at[rows_of(place(me_s), rows)], own_sem.at[1]),
         pltpu.make_async_copy(w_in_ref, w_in_all.at[rows_of(me_c, slab)], own_sem.at[2]),
         pltpu.make_async_copy(w_out_ref, w_out_all.at[me_c], own_sem.at[3]),
     ]
@@ -146,27 +152,39 @@
         part[c] = product[8 * c : 8 * c + 8]
     pl.semaphore_wait(barrier, nc - 1 + ns - 1)
 
-    lat = [
-        remote(latent_ref, lat_all.at[rows_of(me_s, rows)], lat_s.at[k], lat_r.at[k], me_c, seq_peer(k))
-        for k in range(1, ns)
-    ]
+    def seq_gather(src, whole, send, recv):
+        mine_there = whole.at[rows_of(place(me_s), rows)]
+        first = [remote(src, mine_there, send.at[0], recv.at[0], me_c, near)]
+        for j in range(1, far):
+            first.append(remote(src, mine_there, send.at[j], recv.at[j], me_c, seq_peer(2 * j)))
+        return first
+
+    def seq_forward(first, whole, send, recv):
+        second = []
+        for j in range(1, far):
+            first[j].wait_recv()
+            held = whole.at[rows_of(place(seq_peer(ns - 2 * j)), rows)]
+            second.append(remote(held, held, send.at[far + j], recv.at[far + j], me_c, near))
+        return second
+
+    lat = seq_gather(latent_ref, lat_all, lat_s, lat_r)
     m1 = []
     for k in range(1, nc):
         peer = lax.rem(me_c + k, nc)
         m1.append(remote(part.at[peer], part_in.at[me_c], m1_s.at[k], m1_r.at[k], peer, me_s))
 
-    def cand_gather(src, place, send, recv):
-        first = [remote(src, place(me_c), send.at[0], recv.at[0], mate, me_s)]
+    def cand_gather(src, spot, send, recv):
+        first = [remote(src, spot(me_c), send.at[0], recv.at[0], mate, me_s)]
         for j in range(1, half):
             peer = lax.rem(me_c + 2 * j, nc)
-            first.append(remote(src, place(me_c), send.at[j], recv.at[j], peer, me_s))
+            first.append(remote(src, spot(me_c), send.at[j], recv.at[j], peer, me_s))
         return first
 
-    def cand_forward(first, place, send, recv):
+    def cand_forward(first, spot, send, recv):
         second = []
         for j in range(1, half):
             first[j].wait_recv()
-            held = place(lax.rem(me_c - 2 * j + nc, nc))
+            held = spot(lax.rem(me_c - 2 * j + nc, nc))
             second.append(remote(held, held, send.at[half + j], recv.at[half + j], mate, me_s))
         return second
 
@@ -190,11 +208,10 @@
         remote(mine, mod_all.at[me_s], m2_s.at[k], m2_r.at[k], me_c, seq_peer(k))
         for k in range(1, ns)
     ]
-    cot = [
-        remote(cot_ref, cot_all.at[rows_of(me_s, rows)], cot_s.at[k], cot_r.at[k], me_c, seq_peer(k))
-        for k in range(1, ns)
-    ]
-    for copy in lat + m2:
+    lat_second = seq_forward(lat, lat_all, lat_s, lat_r)
+    cot = seq_gather(cot_ref, cot_all, cot_s, cot_r)
+    lat[0].wait_recv()
+    for copy in lat_second + m2:
         copy.wait_recv()
     own[0].wait()
     for s in range(ns):
@@ -256,16 +273,27 @@
     for copy in w_out_second:
         copy.wait_recv()
 
-    def scatter(out, into, send, recv, j):
+    def scatter_near(out, into, send, recv, j):
+        away = out.at[j, rows_of(1 - me_y, far * rows)]
+        return remote(away, into.at[j], send.at[j], recv.at[j], me_c, near)
+
+    def scatter_far(first, out, into, sums, landed, send, recv, j):
+        first.wait_recv()
+        here = out[j, rows_of(me_y, far * rows)].astype(jnp.float32)
+        sums[j] = (here + into[j].astype(jnp.float32)).astype(jnp.bfloat16)
         copies = []
-        for k in range(1, ns):
-            peer = seq_peer(k)
+        for k in range(1, far):
+            peer = lax.rem(me_z + k, far)
             copies.append(
-                remote(out.at[j, rows_of(peer, rows)], into.at[j, me_s], send.at[j, k], recv.at[j, k], me_c, peer)
+                remote(
+                    sums.at[j, rows_of(peer, rows)], landed.at[j, me_z],
+                    send.at[j, k], recv.at[j, k], me_c, 2 * peer + me_y,
+                )
             )
         return copies
 
-    mixed = []
+    cot_second = seq_forward(cot, cot_all, cot_s, cot_r)
+    mixed_near = []
     per_chunk = chunk // piece
     for j in range(CHUNKS):
         for i in range(per_chunk):
@@ -276,9 +304,10 @@
                     att[h], w_out_all[c, h * HEAD : (h + 1) * HEAD], preferred_element_type=jnp.float32
                 )
             mix_out[j, :, i * piece : (i + 1) * piece] = block.astype(jnp.bfloat16)
-        mixed.append(scatter(mix_out, mix_in, mx_s, mx_r, j))
-
-    for copy in cot:
+        mixed_near.append(scatter_near(mix_out, mix_near, mxn_s, mxn_r, j))
+
+    cot[0].wait_recv()
+    for copy in cot_second:
         copy.wait_recv()
     own[1].wait()
 
@@ -321,7 +350,8 @@
 
     lax.fori_loop(0, groups, head_backward, 0)
 
-    d_mod = []
+    d_near = []
+    mixed = []
     for j in range(CHUNKS):
         block = jnp.zeros((length, chunk), jnp.float32)
         for h in range(groups):
@@ -329,13 +359,20 @@
                 d_proj[h], w_in_all[j * chunk : (j + 1) * chunk, h * tile : (h + 1) * tile]
             )
         dm_out[j] = block.astype(jnp.bfloat16)
-        d_mod.append(scatter(dm_out, dm_in, dm_s, dm_r, j))
-
-    def summed(out, into, j, at):
-        start = pl.multiple_of(me_s * rows, rows) + at
-        result = out[j, pl.ds(pl.multiple_of(start, 16), 16)].astype(jnp.float32)
-        for k in range(1, ns):
-            result = result + into[j, lax.rem(me_s + k, ns), at : at + 16].astype(jnp.float32)
+        d_near.append(scatter_near(dm_out, dm_near, dmn_s, dmn_r, j))
+        mixed.append(
+            scatter_far(mixed_near[j], mix_out, mix_near, mix_sum, mix_in, mx_s, mx_r, j)
+        )
+    d_mod = [
+        scatter_far(d_near[j], dm_out, dm_near, dm_sum, dm_in, dm_s, dm_r, j)
+        for j in range(CHUNKS)
+    ]
+
+    def summed(sums, landed, j, at):
+        start = pl.multiple_of(me_z * rows, rows) + at
+        result = sums[j, pl.ds(pl.multiple_of(start, 16), 16)].astype(jnp.float32)
+        for k in range(1, far):
+            result = result + landed[j, lax.rem(me_z + k, far), at : at + 16].astype(jnp.float32)
         return result
 
     for j in range(CHUNKS):
@@ -344,20 +381,20 @@
     for at in range(0, rows, 16):
         for j in range(CHUNKS):
             part_cols = slice(j * chunk, (j + 1) * chunk)
-            own_rows = pl.ds(pl.multiple_of(me_s * rows + at, 16), 16)
+            own_rows = pl.ds(pl.multiple_of(place(me_s) * rows + at, 16), 16)
             block_ref[at : at + 16, part_cols] = (
                 lat_all[own_rows, part_cols].astype(jnp.float32)
-                + vecs[2, 0:1, part_cols] * summed(mix_out, mix_in, j, at)
+                + vecs[2, 0:1, part_cols] * summed(mix_sum, mix_in, j, at)
             ).astype(jnp.bfloat16)
 
     for j in range(CHUNKS):
         for copy in d_mod[j]:
             copy.wait_recv()
     for at in range(0, rows, 16):
-        own_rows = pl.ds(pl.multiple_of(me_s * rows + at, 16), 16)
+        own_rows = pl.ds(pl.multiple_of(place(me_s) * rows + at, 16), 16)
         normed, inverse_std = layer_norm(lat_all[own_rows].astype(jnp.float32))
         d_normed = jnp.concatenate(
-            [summed(dm_out, dm_in, j, at) for j in range(CHUNKS)], axis=1
+            [summed(dm_sum, dm_in, j, at) for j in range(CHUNKS)], axis=1
         ) * (1.0 + vecs[1, 0:1])
         grad_ref[at : at + 16] = cot_all[own_rows].astype(jnp.float32) + inverse_std * (
             d_normed
@@ -365,7 +402,10 @@
             - normed * jnp.mean(d_normed * normed, -1, keepdims=True)
         )
 
-    for copy in lat + m1 + m2 + cot + w_in + w_out + w_in_second + w_out_second:
+    for copy in (
+        lat + lat_second + m1 + m2 + cot + cot_second + w_in + w_out + w_in_second + w_out_second
+        + mixed_near + d_near
+    ):
         copy.wait_send()
     for j in range(CHUNKS):
         for copy in mixed[j] + d_mod[j]:
@@ -385,7 +425,8 @@
     time_act = jax.nn.silu(time_embed(timesteps, width)).astype(jnp.bfloat16)
     act_rows = lax.dynamic_slice_in_dim(time_act, lax.axis_index("cand") * slab, slab, 1)
     act_rows = jnp.repeat(act_rows, 8, axis=0)
-    cos_tab, sin_tab, _swapped, sign_vec = rope_tables(positions, HEAD)
+    ordered = positions.reshape(-1, ns // 2, 2, rows).swapaxes(1, 2).reshape(-1, length)
+    cos_tab, sin_tab, _swapped, sign_vec = rope_tables(ordered, HEAD)
     vmem = pl.BlockSpec(memory_space=pltpu.VMEM)
     anywhere = pl.BlockSpec(memory_space=pl.ANY)
     f32, bf16 = jnp.float32, jnp.bfloat16
@@ -418,14 +459,19 @@
             pltpu.VMEM((groups, length, HEAD), bf16),
             pltpu.VMEM((groups, length, 3 * HEAD), bf16),
             pltpu.VMEM((CHUNKS, length, chunk), bf16),
-            pltpu.VMEM((CHUNKS, ns, rows, chunk), bf16),
+            pltpu.VMEM((CHUNKS, length // 2, chunk), bf16),
+            pltpu.VMEM((CHUNKS, length // 2, chunk), bf16),
+            pltpu.VMEM((CHUNKS, ns // 2, rows, chunk), bf16),
             pltpu.VMEM((CHUNKS, length, chunk), bf16),
-            pltpu.VMEM((CHUNKS, ns, rows, chunk), bf16),
+            pltpu.VMEM((CHUNKS, length // 2, chunk), bf16),
+            pltpu.VMEM((CHUNKS, length // 2, chunk), bf16),
+            pltpu.VMEM((CHUNKS, ns // 2, rows, chunk), bf16),
             dma((4,)),
             dma((ns,)), dma((ns,)), dma((ns,)), dma((ns,)),
             dma((nc,)), dma((nc,)), dma((nc,)), dma((nc,)),
             dma((nc,)), dma((nc,)), dma((ns,)), dma((ns,)),
-            dma((CHUNKS, ns)), dma((CHUNKS, ns)), dma((CHUNKS, ns)), dma((CHUNKS, ns)),
+            dma((CHUNKS,)), dma((CHUNKS,)), dma((CHUNKS, ns // 2)), dma((CHUNKS, ns // 2)),
+            dma((CHUNKS,)), dma((CHUNKS,)), dma((CHUNKS, ns // 2)), dma((CHUNKS, ns // 2)),
         ],
         compiler_params=pltpu.CompilerParams(
             collective_id=0, has_side_effects=True, vmem_limit_bytes=66000000

time: 229 us -> 156 us (0.68)
  Pallas kernels: 218 us -> 145 us
    pallas_call x1, Pallas kernels: 218 us -> 145 us  [on_device(): pl.pallas_call(functools.partial(step_kernel, nc, ns), out_shape=(jax.Sha...]
where the time goes in v3:
time: 156 us
  Pallas kernels  145 us (93%)
  local copies, waits for them, and re-layouts  6.88 us (4%)
  other arithmetic  2.72 us (2%)
    pallas_call x1, Pallas kernels, on_device(): pl.pallas_call(functools.partial(step_kernel, nc, ns), out_shape=(jax.Sha...  145 us
    unnamed x7, local copies, waits for them, and re-layouts  4.88 us

profile of v3, /device:TPU:0, one launch (start us, length us, event | category | flops | bytes accessed | tf_op | source)
XLA Modules:
  0.0 155.7 jit_solution(10652293216282498567)
XLA Ops:
  0.6 0.0 copy-start.1
  0.6 0.7 convert_element_type.36
  1.3 0.8 reshape.59
  2.2 0.1 convert_element_type.43
  2.2 0.1 convert_element_type.41
  2.3 0.1 convert_element_type.39
  2.4 0.3 multiply_cosine_fusion
  2.7 0.6 broadcast_bitcast_fusion.act_ref
  3.4 0.1 broadcast_multiply_fusion.2
  3.5 0.0 copy-start
  3.5 0.2 broadcast_multiply_fusion
  3.7 0.3 concatenate.7
  4.0 0.0 copy-done.1
  4.0 1.4 sine_multiply_fusion
  5.4 0.0 copy-done
  5.5 1.3 copy.11
  6.7 145.3 %shard_map.95 = (bf16[48,3072]{1,0:T(8,128)(2,1)}, f32[48,3072]{1,0:T(8,128)}) custom-call(bf16[32,768]{1,0:T(8,128)(2,1)} %broadcast_bitcast_fusion.act_ref, f32[384,128]{1,0:T(8,128)} %get-tuple-element.7.cos_ref, f32[384,128]{1,0:T(8,128)} %get-tuple-element.6.sin_ref, bf16[768,1152]{1,0:T(8,128)(2,1)} %mod_w_ref.1, bf16[48,3072]{1,0:T(8,128)(2,1)} %bitcast.16, ...), custom_call_target="tpu_custom_call" | custom-call | tf_op jit(solution)/shard_map/pallas_call | solution.py:434
  152.0 1.7 %copy.16 = bf16[1,48,3072]{2,1,0:T(8,128)(2,1)} copy(bf16[1,48,3072]{2,1,0:T(8,128)(2,1)} %bitcast.18) | data formatting | bytes 589824
  153.7 1.9 %copy.17 = f32[1,48,3072]{2,1,0:T(8,128)} copy(f32[1,48,3072]{2,1,0:T(8,128)} %bitcast.14) | data formatting | bytes 1179648
  (6 shorter events, 0.1 us)
Async XLA Ops:
  0.6 3.4 %copy-start.1 = (f32[128]{0:T(128)S(1)}, f32[128]{0:T(128)}, u32[]{:S(2)}) copy-start(f32[128]{0:T(128)} %constant.31.clone) | copy-start | bytes 1540
  3.5 2.0 %copy-start = (bf16[768,2,384]{2,1,0:T(2,128)(2,1)S(1)}, bf16[768,2,384]{2,1,0:T(2,128)(2,1)}, u32[]{:S(2)}) copy-start(bf16[768,2,384]{2,1,0:T(2,128)(2,1)} %param.12) | copy-start | bytes 3538948

commit v4 on v3

--- a/solution.py
+++ b/solution.py
@@ -9,7 +9,8 @@
 from jax.sharding import PartitionSpec as P
 
 HEAD = 128
-CHUNKS = 4
+CHUNKS = 8
+PIECE = 16
 MESH = pl.DeviceIdType.MESH
 
 
@@ -152,22 +153,38 @@
         part[c] = product[8 * c : 8 * c + 8]
     pl.semaphore_wait(barrier, nc - 1 + ns - 1)
 
+    pieces = rows // PIECE
+
+    def piece_of(whole, index, p):
+        return whole.at[pl.ds(pl.multiple_of(place(index) * rows + p * PIECE, PIECE), PIECE)]
+
     def seq_gather(src, whole, send, recv):
-        mine_there = whole.at[rows_of(place(me_s), rows)]
-        first = [remote(src, mine_there, send.at[0], recv.at[0], me_c, near)]
-        for j in range(1, far):
-            first.append(remote(src, mine_there, send.at[j], recv.at[j], me_c, seq_peer(2 * j)))
-        return first
-
-    def seq_forward(first, whole, send, recv):
+        near_copies, far_copies = [], []
+        for p in range(pieces):
+            from_here = src.at[pl.ds(p * PIECE, PIECE)]
+            there = piece_of(whole, me_s, p)
+            near_copies.append(
+                remote(from_here, there, send.at[p, 0], recv.at[p, 0], me_c, near)
+            )
+            far_copies.append(
+                [
+                    remote(from_here, there, send.at[p, j], recv.at[p, j], me_c, seq_peer(2 * j))
+                    for j in range(1, far)
+                ]
+            )
+        return near_copies, far_copies
+
+    def seq_forward(far_copies, whole, send, recv, p):
         second = []
         for j in range(1, far):
-            first[j].wait_recv()
-            held = whole.at[rows_of(place(seq_peer(ns - 2 * j)), rows)]
-            second.append(remote(held, held, send.at[far + j], recv.at[far + j], me_c, near))
+            far_copies[p][j - 1].wait_recv()
+            held = piece_of(whole, seq_peer(ns - 2 * j), p)
+            second.append(
+                remote(held, held, send.at[p, far + j], recv.at[p, far + j], me_c, near)
+            )
         return second
 
-    lat = seq_gather(latent_ref, lat_all, lat_s, lat_r)
+    lat_near, lat_far = seq_gather(latent_ref, lat_all, lat_s, lat_r)
     m1 = []
     for k in range(1, nc):
         peer = lax.rem(me_c + k, nc)
@@ -208,10 +225,12 @@
         remote(mine, mod_all.at[me_s], m2_s.at[k], m2_r.at[k], me_c, seq_peer(k))
         for k in range(1, ns)
     ]
-    lat_second = seq_forward(lat, lat_all, lat_s, lat_r)
-    cot = seq_gather(cot_ref, cot_all, cot_s, cot_r)
-    lat[0].wait_recv()
-    for copy in lat_second + m2:
+    lat_second = []
+    for p in range(pieces):
+        lat_second += seq_forward(lat_far, lat_all, lat_s, lat_r, p)
+    cot_near, cot_far = seq_gather(cot_ref, cot_all, cot_s, cot_r)
+    cot_second = []
+    for copy in lat_near + lat_second + m2:
         copy.wait_recv()
     own[0].wait()
     for s in range(ns):
@@ -231,6 +250,7 @@
         return 0
 
     lax.fori_loop(0, length // 16, norm_rows, 0)
+    cot_second += seq_forward(cot_far, cot_all, cot_s, cot_r, 0)
     w_in_second = cand_forward(w_in, in_place, wi_s, wi_r)
     w_in[0].wait_recv()
     own[2].wait()
@@ -267,6 +287,8 @@
         return 0
 
     lax.fori_loop(0, groups, head_forward, 0)
+    for p in range(1, pieces - 1):
+        cot_second += seq_forward(cot_far, cot_all, cot_s, cot_r, p)
 
     own[3].wait()
     w_out[0].wait_recv()
@@ -292,22 +314,29 @@
             )
         return copies
 
-    cot_second = seq_forward(cot, cot_all, cot_s, cot_r)
     mixed_near = []
-    per_chunk = chunk // piece
-    for j in range(CHUNKS):
-        for i in range(per_chunk):
-            c = j * per_chunk + i
+    span = max(chunk, piece)
+    for n in range(width // span):
+        for i in range(span // piece):
+            c = n * (span // piece) + i
             block = jnp.zeros((length, piece), jnp.float32)
             for h in range(groups):
                 block = block + jnp.dot(
                     att[h], w_out_all[c, h * HEAD : (h + 1) * HEAD], preferred_element_type=jnp.float32
                 )
-            mix_out[j, :, i * piece : (i + 1) * piece] = block.astype(jnp.bfloat16)
-        mixed_near.append(scatter_near(mix_out, mix_near, mxn_s, mxn_r, j))
-
-    cot[0].wait_recv()
-    for copy in cot_second:
+            block = block.astype(jnp.bfloat16)
+            if piece < chunk:
+                mix_out[n, :, i * piece : (i + 1) * piece] = block
+            else:
+                for m in range(span // chunk):
+                    mix_out[n * (span // chunk) + m] = block[:, m * chunk : (m + 1) * chunk]
+        for m in range(span // chunk):
+            j = n * (span // chunk) + m
+            mixed_near.append(scatter_near(mix_out, mix_near, mxn_s, mxn_r, j))
+        if n == 1:
+            cot_second += seq_forward(cot_far, cot_all, cot_s, cot_r, pieces - 1)
+
+    for copy in cot_near + cot_second:
         copy.wait_recv()
     own[1].wait()
 
@@ -403,7 +432,8 @@
         )
 
     for copy in (
-        lat + lat_second + m1 + m2 + cot + cot_second + w_in + w_out + w_in_second + w_out_second
+        lat_near + lat_second + sum(lat_far, []) + m1 + m2 + cot_near + cot_second
+        + sum(cot_far, []) + w_in + w_out + w_in_second + w_out_second
         + mixed_near + d_near
     ):
         copy.wait_send()
@@ -467,7 +497,8 @@
             pltpu.VMEM((CHUNKS, length // 2, chunk), bf16),
             pltpu.VMEM((CHUNKS, ns // 2, rows, chunk), bf16),
             dma((4,)),
-            dma((ns,)), dma((ns,)), dma((ns,)), dma((ns,)),
+            dma((rows // PIECE, ns)), dma((rows // PIECE, ns)),
+            dma((rows // PIECE, ns)), dma((rows // PIECE, ns)),
             dma((nc,)), dma((nc,)), dma((nc,)), dma((nc,)),
             dma((nc,)), dma((nc,)), dma((ns,)), dma((ns,)),
             dma((CHUNKS,)), dma((CHUNKS,)), dma((CHUNKS, ns // 2)), dma((CHUNKS, ns // 2)),

time: 156 us -> 161 us (1.032)
  Pallas kernels: 145 us -> 151 us
    pallas_call x1, Pallas kernels: 145 us -> 151 us  [on_device(): pl.pallas_call(functools.partial(step_kernel, nc, ns), out_shape=(jax.Sha...]
where the time goes in v4:
time: 161 us
  Pallas kernels  151 us (94%)
  local copies, waits for them, and re-layouts  6.88 us (4%)
  other arithmetic  2.72 us (2%)
    pallas_call x1, Pallas kernels, on_device(): pl.pallas_call(functools.partial(step_kernel, nc, ns), out_shape=(jax.Sha...  151 us
    unnamed x7, local copies, waits for them, and re-layouts  4.88 us

profile of v4, /device:TPU:0, one launch (start us, length us, event | category | flops | bytes accessed | tf_op | source)
XLA Modules:
  0.0 161.1 jit_solution(4369727330630325383)
XLA Ops:
  0.6 0.0 copy-start.1
  0.6 0.7 convert_element_type.36
  1.3 0.8 reshape.59
  2.2 0.1 convert_element_type.43
  2.2 0.1 convert_element_type.41
  2.3 0.1 convert_element_type.39
  2.4 0.3 multiply_cosine_fusion
  2.7 0.6 broadcast_bitcast_fusion.act_ref
  3.4 0.1 broadcast_multiply_fusion.2
  3.5 0.0 copy-start
  3.5 0.2 broadcast_multiply_fusion
  3.7 0.3 concatenate.7
  4.0 0.0 copy-done.1
  4.0 1.4 sine_multiply_fusion
  5.4 0.0 copy-done
  5.5 1.3 copy.11
  6.7 150.7 %shard_map.95 = (bf16[48,3072]{1,0:T(8,128)(2,1)}, f32[48,3072]{1,0:T(8,128)}) custom-call(bf16[32,768]{1,0:T(8,128)(2,1)} %broadcast_bitcast_fusion.act_ref, f32[384,128]{1,0:T(8,128)} %get-tuple-element.7.cos_ref, f32[384,128]{1,0:T(8,128)} %get-tuple-element.6.sin_ref, bf16[768,1152]{1,0:T(8,128)(2,1)} %mod_w_ref.1, bf16[48,3072]{1,0:T(8,128)(2,1)} %bitcast.16, ...), custom_call_target="tpu_custom_call" | custom-call | tf_op jit(solution)/shard_map/pallas_call | solution.py:464
  157.5 1.7 %copy.16 = bf16[1,48,3072]{2,1,0:T(8,128)(2,1)} copy(bf16[1,48,3072]{2,1,0:T(8,128)(2,1)} %bitcast.18) | data formatting | bytes 589824
  159.2 1.9 %copy.17 = f32[1,48,3072]{2,1,0:T(8,128)} copy(f32[1,48,3072]{2,1,0:T(8,128)} %bitcast.14) | data formatting | bytes 1179648
  (6 shorter events, 0.1 us)
Async XLA Ops:
  0.6 3.4 %copy-start.1 = (f32[128]{0:T(128)S(1)}, f32[128]{0:T(128)}, u32[]{:S(2)}) copy-start(f32[128]{0:T(128)} %constant.31.clone) | copy-start | bytes 1540
  3.5 2.0 %copy-start = (bf16[768,2,384]{2,1,0:T(2,128)(2,1)S(1)}, bf16[768,2,384]{2,1,0:T(2,128)(2,1)}, u32[]{:S(2)}) copy-start(bf16[768,2,384]{2,1,0:T(2,128)(2,1)} %param.12) | copy-start | bytes 3538948

commit v5 on v4

--- a/solution.py
+++ b/solution.py
@@ -9,8 +9,8 @@
 from jax.sharding import PartitionSpec as P
 
 HEAD = 128
-CHUNKS = 8
-PIECE = 16
+CHUNKS = 4
+PARTS = 1
 MESH = pl.DeviceIdType.MESH
 
 
@@ -153,15 +153,16 @@
         part[c] = product[8 * c : 8 * c + 8]
     pl.semaphore_wait(barrier, nc - 1 + ns - 1)
 
-    pieces = rows // PIECE
+    pieces = PARTS
+    size = rows // PARTS
 
     def piece_of(whole, index, p):
-        return whole.at[pl.ds(pl.multiple_of(place(index) * rows + p * PIECE, PIECE), PIECE)]
+        return whole.at[pl.ds(pl.multiple_of(place(index) * rows + p * size, size), size)]
 
     def seq_gather(src, whole, send, recv):
         near_copies, far_copies = [], []
         for p in range(pieces):
-            from_here = src.at[pl.ds(p * PIECE, PIECE)]
+            from_here = src.at[pl.ds(p * size, size)]
             there = piece_of(whole, me_s, p)
             near_copies.append(
                 remote(from_here, there, send.at[p, 0], recv.at[p, 0], me_c, near)
@@ -287,7 +288,7 @@
         return 0
 
     lax.fori_loop(0, groups, head_forward, 0)
-    for p in range(1, pieces - 1):
+    for p in range(1, pieces):
         cot_second += seq_forward(cot_far, cot_all, cot_s, cot_r, p)
 
     own[3].wait()
@@ -333,8 +334,6 @@
         for m in range(span // chunk):
             j = n * (span // chunk) + m
             mixed_near.append(scatter_near(mix_out, mix_near, mxn_s, mxn_r, j))
-        if n == 1:
-            cot_second += seq_forward(cot_far, cot_all, cot_s, cot_r, pieces - 1)
 
     for copy in cot_near + cot_second:
         copy.wait_recv()
@@ -497,8 +496,8 @@
             pltpu.VMEM((CHUNKS, length // 2, chunk), bf16),
             pltpu.VMEM((CHUNKS, ns // 2, rows, chunk), bf16),
             dma((4,)),
-            dma((rows // PIECE, ns)), dma((rows // PIECE, ns)),
-            dma((rows // PIECE, ns)), dma((rows // PIECE, ns)),
+            dma((PARTS, ns)), dma((PARTS, ns)),
+            dma((PARTS, ns)), dma((PARTS, ns)),
             dma((nc,)), dma((nc,)), dma((nc,)), dma((nc,)),
             dma((nc,)), dma((nc,)), dma((ns,)), dma((ns,)),
             dma((CHUNKS,)), dma((CHUNKS,)), dma((CHUNKS, ns // 2)), dma((CHUNKS, ns // 2)),

time: 161 us -> 151 us (0.938)
  Pallas kernels: 151 us -> 141 us
    pallas_call x1, Pallas kernels: 151 us -> 141 us  [on_device(): pl.pallas_call(functools.partial(step_kernel, nc, ns), out_shape=(jax.Sha...]
where the time goes in v5:
time: 151 us
  Pallas kernels  141 us (93%)
  local copies, waits for them, and re-layouts  6.88 us (5%)
  other arithmetic  2.72 us (2%)
    pallas_call x1, Pallas kernels, on_device(): pl.pallas_call(functools.partial(step_kernel, nc, ns), out_shape=(jax.Sha...  141 us
    unnamed x7, local copies, waits for them, and re-layouts  4.88 us

profile of v5, /device:TPU:0, one launch (start us, length us, event | category | flops | bytes accessed | tf_op | source)
XLA Modules:
  0.0 151.0 jit_solution(12304051951037472415)
XLA Ops:
  0.6 0.0 copy-start.1
  0.6 0.7 convert_element_type.36
  1.3 0.8 reshape.59
  2.2 0.1 convert_element_type.43
  2.2 0.1 convert_element_type.41
  2.3 0.1 convert_element_type.39
  2.4 0.3 multiply_cosine_fusion
  2.7 0.6 broadcast_bitcast_fusion.act_ref
  3.4 0.1 broadcast_multiply_fusion.2
  3.5 0.0 copy-start
  3.5 0.2 broadcast_multiply_fusion
  3.7 0.3 concatenate.7
  4.0 0.0 copy-done.1
  4.0 1.4 sine_multiply_fusion
  5.4 0.0 copy-done
  5.5 1.3 copy.11
  6.7 140.7 %shard_map.95 = (bf16[48,3072]{1,0:T(8,128)(2,1)}, f32[48,3072]{1,0:T(8,128)}) custom-call(bf16[32,768]{1,0:T(8,128)(2,1)} %broadcast_bitcast_fusion.act_ref, f32[384,128]{1,0:T(8,128)} %get-tuple-element.7.cos_ref, f32[384,128]{1,0:T(8,128)} %get-tuple-element.6.sin_ref, bf16[768,1152]{1,0:T(8,128)(2,1)} %mod_w_ref.1, bf16[48,3072]{1,0:T(8,128)(2,1)} %bitcast.16, ...), custom_call_target="tpu_custom_call" | custom-call | tf_op jit(solution)/shard_map/pallas_call | solution.py:463
  147.4 1.7 %copy.16 = bf16[1,48,3072]{2,1,0:T(8,128)(2,1)} copy(bf16[1,48,3072]{2,1,0:T(8,128)(2,1)} %bitcast.18) | data formatting | bytes 589824
  149.1 1.9 %copy.17 = f32[1,48,3072]{2,1,0:T(8,128)} copy(f32[1,48,3072]{2,1,0:T(8,128)} %bitcast.14) | data formatting | bytes 1179648
  (6 shorter events, 0.1 us)
Async XLA Ops:
  0.6 3.4 %copy-start.1 = (f32[128]{0:T(128)S(1)}, f32[128]{0:T(128)}, u32[]{:S(2)}) copy-start(f32[128]{0:T(128)} %constant.31.clone) | copy-start | bytes 1540
  3.5 2.0 %copy-start = (bf16[768,2,384]{2,1,0:T(2,128)(2,1)S(1)}, bf16[768,2,384]{2,1,0:T(2,128)(2,1)}, u32[]{:S(2)}) copy-start(bf16[768,2,384]{2,1,0:T(2,128)(2,1)} %param.12) | copy-start | bytes 3538948
